TPU v7x, 32 devices: a whole 2x2x4 slice. The times are simulated.
32 devices in a mesh: row: 4 (over x, core), col: 2 (over y), fiber: 4 (over z).
Axes of the slice: x: 2, y: 2, z: 4, core: 2. Of those that a mesh axis runs over, the one named last changes fastest.
Arguments:
- values: float32 [3072, 3072], P('row', ('col', 'fiber')), may hold values from -6 to 6
- tile_mask: int32 [24, 24], P('row', ('col', 'fiber')), may hold values from 0 to 1, as said below
- keep_mask: int32 [24, 24], P('row', ('col', 'fiber')), may hold values 0 or 1
Outputs:
- flows: float32 [3072, 3072], P('row', ('col', 'fiber'))
Inputs may be any that keep to these rules, and one draw needn't show every extreme that they name: `tile_mask`: 1 marks a tile that holds entries; every diagonal tile is 1, and tiles with low indices are denser.
All inputs are finite; a program needn't handle non-finite values. No bound on the sum of `keep_mask` on one device may be relied on, other than what follows from the above.
Results may differ from a plain program's by a relative error of at most 0.017.
Values may be sent and summed in bfloat16 or wider, within the bound.
A program may use at most 64 MiB of HBM per device.

v0:
```python
import functools

import jax
import jax.numpy as jnp
from jax import lax
from jax.experimental import pallas as pl
from jax.experimental.pallas import tpu as pltpu
from jax.sharding import PartitionSpec as P

MESH = pl.DeviceIdType.MESH
CHUNKS = 6
EARLY = 3
BLOCKS = 3
LAG = 2
VMEM_LIMIT = 62 * 1024 * 1024


def kernel(
    n_row, n_col, n_fib, tile_hbm, values_hbm, own, inverse_ref,
    tile_ref, values_ref, left, right, ahead, part_out, part_in, sums, load_sem,
    send_up, send_down, recv_left, send_right, recv_right, send_pair, recv_pair,
    send_part, recv_part, send_sum, recv_sum,
):
    r, c, f = lax.axis_index("row"), lax.axis_index("col"), lax.axis_index("fiber")
    rows, unit = values_ref.shape
    tile = unit // tile_ref.shape[0]
    step = rows // CHUNKS
    group = n_row // n_col
    owner, seat = r // group, lax.rem(r, group)

    load = pltpu.make_async_copy(values_hbm, values_ref, load_sem.at[0])
    load.start()
    load_tile = pltpu.make_async_copy(tile_hbm, tile_ref, load_sem.at[1])
    load_tile.start()

    barrier = pltpu.get_barrier_semaphore()
    for dr in range(n_row):
        for dc in range(n_col):
            if dr or dc:
                pl.semaphore_signal(
                    barrier, inc=1, device_id_type=MESH,
                    device_id=(lax.rem(r + dr, n_row), lax.rem(c + dc, n_col), f),
                )

    has_down, has_up = f > 0, f < n_fib - 1

    @pl.when(has_down)
    def _():
        pl.semaphore_signal(barrier, inc=1, device_id=(r, c, f - 1), device_id_type=MESH)

    @pl.when(has_up)
    def _():
        pl.semaphore_signal(barrier, inc=1, device_id=(r, c, f + 1), device_id_type=MESH)

    load_tile.wait()
    load.wait()

    for i in range(rows // tile):
        for j in range(unit // tile):
            at = (pl.ds(i * tile, tile), pl.ds(j * tile, tile))
            masked = values_ref[at] * tile_ref[j, i].astype(jnp.float32)
            left[f, i * tile:(i + 1) * tile, j * tile:(j + 1) * tile] = masked.astype(jnp.bfloat16)

    neighbours = has_down.astype(jnp.int32) + has_up.astype(jnp.int32)
    pl.semaphore_wait(barrier, n_row * n_col - 1 + neighbours)

    def along(source, i, up):
        part = left.at[source, pl.ds(pl.multiple_of(i * step, step), step)]
        return pltpu.make_async_remote_copy(
            src_ref=part, dst_ref=part,
            send_sem=(send_up if up else send_down).at[source, i],
            recv_sem=recv_left.at[source, i],
            device_id=(r, c, f + 1 if up else f - 1), device_id_type=MESH,
        )

    def right_at(col, place):
        return right.at[
            pl.ds(pl.multiple_of(place * rows, rows), rows),
            pl.ds(pl.multiple_of(col * unit, unit), unit),
        ]

    def to_right(t):
        return pltpu.make_async_remote_copy(
            src_ref=left.at[f], dst_ref=right_at(c, seat),
            send_sem=send_right.at[t], recv_sem=recv_right.at[c],
            device_id=(t * group + seat, owner, f), device_id_type=MESH,
        )

    def came_right(col):
        return pltpu.make_async_remote_copy(
            src_ref=left.at[f], dst_ref=right_at(col, seat),
            send_sem=send_right.at[0], recv_sem=recv_right.at[col],
            device_id=(r, c, f), device_id_type=MESH,
        )

    def to_pair(col, other):
        return pltpu.make_async_remote_copy(
            src_ref=right_at(col, seat), dst_ref=right_at(col, seat),
            send_sem=send_pair.at[col, other], recv_sem=recv_pair.at[col, seat],
            device_id=(owner * group + other, c, f), device_id_type=MESH,
        )

    def came_pair(col, other):
        return pltpu.make_async_remote_copy(
            src_ref=right_at(col, other), dst_ref=right_at(col, other),
            send_sem=send_pair.at[col, other], recv_sem=recv_pair.at[col, other],
            device_id=(r, c, f), device_id_type=MESH,
        )

    def to_col(col, i):
        part = pl.ds(pl.multiple_of(i * step, step), step)
        return pltpu.make_async_remote_copy(
            src_ref=part_out.at[col, part], dst_ref=part_in.at[c, part],
            send_sem=send_part.at[col, i], recv_sem=recv_part.at[c, i],
            device_id=(r, col, f), device_id_type=MESH,
        )

    def came_col(col, i):
        part = pl.ds(pl.multiple_of(i * step, step), step)
        return pltpu.make_async_remote_copy(
            src_ref=part_out.at[col, part], dst_ref=part_in.at[col, part],
            send_sem=send_part.at[col, i], recv_sem=recv_part.at[col, i],
            device_id=(r, col, f), device_id_type=MESH,
        )

    @pl.loop(0, CHUNKS)
    def _(i):
        @pl.when(has_down)
        def _():
            along(f, i, False).start()

        @pl.when(has_up)
        def _():
            along(f, i, True).start()

    mine = owner == c
    for t in range(n_row // group):
        @pl.when(jnp.logical_not(mine & (owner == t)))
        def _():
            to_right(t).start()

    @pl.when(mine)
    def _():
        spot = right_at(c, seat)
        spot[...] = left[f]

    def relay(d, i):
        @pl.when(f - d >= 0)
        def _():
            along(f - d, i, True).wait_recv()

            @pl.when(has_up)
            def _():
                along(f - d, i, True).start()

        @pl.when(f + d < n_fib)
        def _():
            along(f + d, i, False).wait_recv()

            @pl.when(has_down)
            def _():
                along(f + d, i, False).start()

    def gather_right():
        for col in range(n_col):
            @pl.when(jnp.logical_not(mine & (c == col)))
            def _():
                came_right(col).wait_recv()

            for other in range(group):
                @pl.when(seat != other)
                def _():
                    to_pair(col, other).start()

    up_late, down_late = f + 1 == n_fib - 1, f - 1 == 0

    @pl.loop(0, CHUNKS)
    def _(i):
        @pl.when(has_down)
        def _():
            along(f - 1, i, True).wait_recv()

            @pl.when(has_up & (jnp.logical_not(up_late) | (i < EARLY)))
            def _():
                along(f - 1, i, True).start()

        @pl.when(has_up)
        def _():
            along(f + 1, i, False).wait_recv()

            @pl.when(has_down & (jnp.logical_not(down_late) | (i < EARLY)))
            def _():
                along(f + 1, i, False).start()

    gather_right()

    for col in range(n_col):
        for other in range(group):
            @pl.when(seat != other)
            def _():
                came_pair(col, other).wait_recv()

    first = jnp.where(has_down, f - 1, 0)
    ready = min(n_fib, 2)

    def product(part, shift, k):
        col = lax.rem(c + shift, n_col)
        return jnp.dot(
            left[k, part, :],
            right[
                pl.ds(pl.multiple_of(k * unit, unit), unit),
                pl.ds(pl.multiple_of(col * unit, unit), unit),
            ],
            preferred_element_type=jnp.float32,
        )

    def total_at(shift):
        return own if shift == 0 else ahead.at[shift - 1]

    @pl.loop(0, BLOCKS)
    def _(i):
        part = pl.ds(pl.multiple_of(i * (rows // BLOCKS), rows // BLOCKS), rows // BLOCKS)
        for shift in range(n_col):
            total = jnp.zeros((rows // BLOCKS, unit), jnp.float32)
            for k in range(ready):
                total += product(part, shift, lax.rem(first + k, n_fib))
            total_at(shift)[part, :] = total

    sums[r] = jnp.zeros((8, unit), jnp.float32)

    def combine(i):
        part = pl.ds(pl.multiple_of(i * step, step), step)
        expanded = own[part, :]
        for shift in range(1, n_col):
            col = lax.rem(c + shift, n_col)
            came_col(col, i).wait_recv()
            expanded += part_in[col, part, :].astype(jnp.float32)
        squared = expanded * expanded
        own[part, :] = squared
        sums[r] += jnp.sum(squared.reshape(step // 8, 8, unit), axis=0)

    @pl.loop(0, CHUNKS)
    def _(i):
        @pl.when(has_up & has_down & (i < CHUNKS - EARLY))
        def _():
            @pl.when(up_late)
            def _():
                along(f - 1, i + EARLY, True).start()

            @pl.when(down_late)
            def _():
                along(f + 1, i + EARLY, False).start()

        for d in range(2, n_fib):
            relay(d, i)
        part = pl.ds(pl.multiple_of(i * step, step), step)
        for shift in range(1, n_col):
            col = lax.rem(c + shift, n_col)
            total = ahead[shift - 1, part, :]
            for k in range(ready, n_fib):
                total += product(part, shift, lax.rem(first + k, n_fib))
            part_out[col, part, :] = total.astype(jnp.bfloat16)
            to_col(col, i).start()
        total = own[part, :]
        for k in range(ready, n_fib):
            total += product(part, 0, lax.rem(first + k, n_fib))
        own[part, :] = total

        @pl.when(i >= LAG)
        def _():
            combine(i - LAG)

    @pl.loop(CHUNKS - LAG, CHUNKS)
    def _(i):
        combine(i)

    def to_row(shift):
        return pltpu.make_async_remote_copy(
            src_ref=sums.at[r], dst_ref=sums.at[r],
            send_sem=send_sum.at[shift], recv_sem=recv_sum.at[r],
            device_id=(lax.rem(r + shift, n_row), c, f), device_id_type=MESH,
        )

    def came_row(other):
        return pltpu.make_async_remote_copy(
            src_ref=sums.at[r], dst_ref=sums.at[other],
            send_sem=send_sum.at[0], recv_sem=recv_sum.at[other],
            device_id=(other, c, f), device_id_type=MESH,
        )

    for shift in range(1, n_row):
        to_row(shift).start()
    for shift in range(1, n_row):
        came_row(lax.rem(r + shift, n_row)).wait_recv()
    total = sums[0]
    for other in range(1, n_row):
        total += sums[other]
    scale = jnp.sum(total, axis=0, keepdims=True) / (rows * n_row) + 1e-6
    inverse_ref[...] = jnp.broadcast_to(1.0 / scale, inverse_ref.shape)

    @pl.loop(0, CHUNKS)
    def _(i):
        for source in range(n_fib):
            @pl.when(has_up & (source <= f))
            def _():
                along(source, i, True).wait_send()

            @pl.when(has_down & (source >= f))
            def _():
                along(source, i, False).wait_send()

        for shift in range(1, n_col):
            to_col(lax.rem(c + shift, n_col), i).wait_send()

    for t in range(n_row // group):
        @pl.when(jnp.logical_not(mine & (owner == t)))
        def _():
            to_right(t).wait_send()

    for col in range(n_col):
        for other in range(group):
            @pl.when(seat != other)
            def _():
                to_pair(col, other).wait_send()

    for shift in range(1, n_row):
        to_row(shift).wait_send()


def prune(keep_ref, squared_ref, inverse_ref, out_hbm, out_vmem, sem):
    tile = out_vmem.shape[1] // keep_ref.shape[0]
    copies = []
    for i in range(keep_ref.shape[1]):
        down = slice(i * tile, (i + 1) * tile)
        for j in range(keep_ref.shape[0]):
            across = slice(j * tile, (j + 1) * tile)
            factor = inverse_ref[0:1, across] * keep_ref[j, i].astype(jnp.float32)
            out_vmem[down, across] = squared_ref[down, across] * factor
        copy = pltpu.make_async_copy(out_vmem.at[down], out_hbm.at[down], sem.at[i])
        copy.start()
        copies.append(copy)
    for copy in copies:
        copy.wait()


def solution(mesh):
    n_row, n_col, n_fib = (mesh.shape[name] for name in ("row", "col", "fiber"))
    group = n_row // n_col

    def local(values, tile_mask, keep_mask):
        rows, unit = values.shape
        dma = pltpu.SemaphoreType.DMA
        squared, inverse = pl.pallas_call(
            functools.partial(kernel, n_row, n_col, n_fib),
            out_shape=(
                pltpu.VMEM((rows, unit), jnp.float32),
                pltpu.VMEM((8, unit), jnp.float32),
            ),
            in_specs=[
                pl.BlockSpec(memory_space=pltpu.HBM),
                pl.BlockSpec(memory_space=pltpu.HBM),
            ],
            out_specs=(
                pl.BlockSpec(memory_space=pltpu.VMEM),
                pl.BlockSpec(memory_space=pltpu.VMEM),
            ),
            scratch_shapes=[
                pltpu.SMEM(tile_mask.shape[::-1], jnp.int32),
                pltpu.VMEM((rows, unit), jnp.float32),
                pltpu.VMEM((n_fib, rows, unit), jnp.bfloat16),
                pltpu.VMEM((group * rows, n_col * unit), jnp.bfloat16),
                pltpu.VMEM((n_col - 1, rows, unit), jnp.float32),
                pltpu.VMEM((n_col, rows, unit), jnp.bfloat16),
                pltpu.VMEM((n_col, rows, unit), jnp.bfloat16),
                pltpu.VMEM((n_row, 8, unit), jnp.float32),
                dma((2,)),
                dma((n_fib, CHUNKS)),
                dma((n_fib, CHUNKS)),
                dma((n_fib, CHUNKS)),
                dma((n_row // group,)),
                dma((n_col,)),
                dma((n_col, group)),
                dma((n_col, group)),
                dma((n_col, CHUNKS)),
                dma((n_col, CHUNKS)),
                dma((n_row,)),
                dma((n_row,)),
            ],
            compiler_params=pltpu.CompilerParams(
                collective_id=0, has_side_effects=True, vmem_limit_bytes=VMEM_LIMIT
            ),
            name="expand",
        )(tile_mask.T, values)
        return pl.pallas_call(
            prune,
            out_shape=jax.ShapeDtypeStruct((rows, unit), jnp.float32),
            in_specs=[
                pl.BlockSpec(memory_space=pltpu.SMEM),
                pl.BlockSpec(memory_space=pltpu.VMEM),
                pl.BlockSpec(memory_space=pltpu.VMEM),
            ],
            out_specs=pl.BlockSpec(memory_space=pl.ANY),
            scratch_shapes=[
                pltpu.VMEM((rows, unit), jnp.float32),
                dma((keep_mask.shape[0],)),
            ],
            compiler_params=pltpu.CompilerParams(vmem_limit_bytes=8 * 1024 * 1024),
            name="prune",
        )(keep_mask.T, squared, inverse)

    spec = P("row", ("col", "fiber"))
    return jax.shard_map(
        local, mesh=mesh, in_specs=(spec, spec, spec), out_specs=spec, check_vma=False
    )
```

profile of v0, /device:TPU:0, one launch (start us, length us, event | category | flops | bytes accessed | tf_op | source)
XLA Modules:
  0.0 53.0 jit_solution(5466376979949230586)
XLA Ops:
  0.0 0.0 copy-start
  0.0 51.4 %expand.1 = (f32[768,384]{1,0:T(8,128)S(1)}, f32[8,384]{1,0:T(8,128)S(1)}) custom-call(s32[3,6]{1,0:T(4,128)} %bitcast.3, f32[768,384]{1,0:T(8,128)} %values_hbm.1), custom_call_target="tpu_custom_call" | custom-call | tf_op jit(solution)/shard_map/expand/pallas_call | solution.py:353
  51.4 0.0 copy-done
  51.4 1.6 %prune.1 = f32[768,384]{1,0:T(8,128)} custom-call(s32[3,6]{1,0:T(4,128)S(1)} %bitcast.2, f32[768,384]{1,0:T(8,128)S(1)} %get-tuple-element.7.squared_ref, f32[8,384]{1,0:T(8,128)S(1)} %get-tuple-element.8.inverse_ref), custom_call_target="tpu_custom_call" | custom-call | tf_op jit(solution)/shard_map/prune/pallas_call | solution.py:394
Async XLA Ops:
  0.0 51.4 %copy-start = (s32[6,3]{0,1:T(4,128)S(1)}, s32[6,3]{0,1:T(4,128)}, u32[]{:S(2)}) copy-start(s32[6,3]{0,1:T(4,128)} %param.5) | copy-start | bytes 220
where the time goes:
time: 53.2 us; the launch traced here: 53 us
  Pallas kernels  53 us (100%)
    pallas_call x1, Pallas kernels, local(): pl.pallas_call(functools.partial(kernel, n_row, n_col, n_fib), out_shape=...  51.4 us
    pallas_call x1, Pallas kernels, local(): pl.pallas_call(prune, out_shape=jax.ShapeDtypeStruct((rows, unit), jnp.fl...  1.64 us

commit v1 on v0

v1 whole, which is shorter than its diff:
```python
import functools

import jax
import jax.numpy as jnp
from jax import lax
from jax.experimental import pallas as pl
from jax.experimental.pallas import tpu as pltpu
from jax.sharding import PartitionSpec as P

MESH = pl.DeviceIdType.MESH
CHUNKS = 8
HELP = 2
FETCH = 6
ANSWER = 7
LAG = 2
VMEM_LIMIT = 62 * 1024 * 1024


def kernel(
    n_row, n_col, n_fib, helps, tile_hbm, values_hbm, own, inverse_ref,
    tile_ref, values_ref, left, right, ahead, part_out, part_in, sums,
    right_far, help_own, help_out, help_in, helped, load_sem,
    send_up, send_down, recv_left, send_right, recv_right, send_pair, recv_pair,
    send_part, recv_part, send_sum, recv_sum,
    send_far, send_side, recv_far, send_far_pair, recv_far_pair,
    send_help, recv_help, send_done, recv_done,
):
    r, c, f = lax.axis_index("row"), lax.axis_index("col"), lax.axis_index("fiber")
    rows, unit = values_ref.shape
    tile = unit // tile_ref.shape[0]
    step = rows // CHUNKS
    parts = rows // unit
    group = n_row // n_col
    owner, seat = r // group, lax.rem(r, group)

    load = pltpu.make_async_copy(values_hbm, values_ref, load_sem.at[0])
    load.start()
    load_tile = pltpu.make_async_copy(tile_hbm, tile_ref, load_sem.at[1])
    load_tile.start()

    barrier = pltpu.get_barrier_semaphore()
    for dr in range(n_row):
        for dc in range(n_col):
            if dr or dc:
                pl.semaphore_signal(
                    barrier, inc=1, device_id_type=MESH,
                    device_id=(lax.rem(r + dr, n_row), lax.rem(c + dc, n_col), f),
                )

    has_down, has_up = f > 0, f < n_fib - 1
    outer = jnp.logical_not(has_down & has_up)
    helper = (f == 1) | (f == n_fib - 2)
    mate = jnp.where(outer, jnp.where(has_down, f - 1, 1), jnp.where(f == 1, 0, n_fib - 1))
    mine = owner == c

    @pl.when(has_down)
    def _():
        pl.semaphore_signal(barrier, inc=1, device_id=(r, c, f - 1), device_id_type=MESH)

    @pl.when(has_up)
    def _():
        pl.semaphore_signal(barrier, inc=1, device_id=(r, c, f + 1), device_id_type=MESH)

    load_tile.wait()
    load.wait()

    for i in range(rows // tile):
        for j in range(unit // tile):
            at = (pl.ds(i * tile, tile), pl.ds(j * tile, tile))
            masked = values_ref[at] * tile_ref[j, i].astype(jnp.float32)
            left[f, i * tile:(i + 1) * tile, j * tile:(j + 1) * tile] = masked.astype(jnp.bfloat16)

    neighbours = has_down.astype(jnp.int32) + has_up.astype(jnp.int32)
    pl.semaphore_wait(barrier, n_row * n_col - 1 + neighbours)

    def chunk(i):
        return pl.ds(pl.multiple_of(i * step, step), step)

    def along(source, i, up):
        part = left.at[source, chunk(i)]
        return pltpu.make_async_remote_copy(
            src_ref=part, dst_ref=part,
            send_sem=(send_up if up else send_down).at[source, i],
            recv_sem=recv_left.at[source, i],
            device_id=(r, c, f + 1 if up else f - 1), device_id_type=MESH,
        )

    def sends_up(i):
        return has_up & ((i >= helps) | (f + 1 < n_fib - 1))

    def sends_down(i):
        return has_down & ((i >= helps) | (f - 1 > 0))

    def gets_up(i):
        return (i >= helps) | has_up

    def gets_down(i):
        return (i >= helps) | has_down

    def right_at(ref, col, place, b):
        return ref.at[
            pl.ds(pl.multiple_of(place * rows + b * unit, unit), unit),
            pl.ds(pl.multiple_of(col * unit, unit), unit),
        ]

    def block(source, b):
        return left.at[source, pl.ds(b * unit, unit)]

    def to_right(t, b):
        return pltpu.make_async_remote_copy(
            src_ref=block(f, b), dst_ref=right_at(right, c, seat, b),
            send_sem=send_right.at[t, b], recv_sem=recv_right.at[c, b],
            device_id=(t * group + seat, owner, f), device_id_type=MESH,
        )

    def came_right(col, b):
        return pltpu.make_async_remote_copy(
            src_ref=block(f, b), dst_ref=right_at(right, col, seat, b),
            send_sem=send_right.at[0, b], recv_sem=recv_right.at[col, b],
            device_id=(r, c, f), device_id_type=MESH,
        )

    def to_far(col, b):
        return pltpu.make_async_remote_copy(
            src_ref=right_at(right, col, seat, b), dst_ref=right_at(right_far, col, seat, b),
            send_sem=send_far.at[col, b], recv_sem=recv_far.at[col, b],
            device_id=(r, c, mate), device_id_type=MESH,
        )

    def to_side(t, b):
        return pltpu.make_async_remote_copy(
            src_ref=block(mate, b), dst_ref=right_at(right_far, c, seat, b),
            send_sem=send_side.at[t, b], recv_sem=recv_far.at[c, b],
            device_id=(t * group + seat, c, f), device_id_type=MESH,
        )

    def came_far(col, b):
        return pltpu.make_async_remote_copy(
            src_ref=block(f, b), dst_ref=right_at(right_far, col, seat, b),
            send_sem=send_far.at[col, b], recv_sem=recv_far.at[col, b],
            device_id=(r, c, f), device_id_type=MESH,
        )

    def pairing(ref, sends, recvs):
        def to_pair(col, b, other):
            return pltpu.make_async_remote_copy(
                src_ref=right_at(ref, col, seat, b), dst_ref=right_at(ref, col, seat, b),
                send_sem=sends.at[col, b, other], recv_sem=recvs.at[col, b, seat],
                device_id=(owner * group + other, c, f), device_id_type=MESH,
            )

        def came_pair(col, b, other):
            return pltpu.make_async_remote_copy(
                src_ref=right_at(ref, col, other, b), dst_ref=right_at(ref, col, other, b),
                send_sem=sends.at[col, b, other], recv_sem=recvs.at[col, b, other],
                device_id=(r, c, f), device_id_type=MESH,
            )

        return to_pair, came_pair

    to_pair, came_pair = pairing(right, send_pair, recv_pair)
    to_far_pair, came_far_pair = pairing(right_far, send_far_pair, recv_far_pair)

    def crossing(out, into, sends, recvs):
        def to_col(col, i):
            return pltpu.make_async_remote_copy(
                src_ref=out.at[col, chunk(i)], dst_ref=into.at[c, chunk(i)],
                send_sem=sends.at[col, i], recv_sem=recvs.at[c, i],
                device_id=(r, col, f), device_id_type=MESH,
            )

        def came_col(col, i):
            return pltpu.make_async_remote_copy(
                src_ref=out.at[col, chunk(i)], dst_ref=into.at[col, chunk(i)],
                send_sem=sends.at[col, i], recv_sem=recvs.at[col, i],
                device_id=(r, col, f), device_id_type=MESH,
            )

        return to_col, came_col

    to_col, came_col = crossing(part_out, part_in, send_part, recv_part)
    to_help, came_help = crossing(help_out, help_in, send_help, recv_help)

    def to_done(i):
        return pltpu.make_async_remote_copy(
            src_ref=helped.at[chunk(i)], dst_ref=helped.at[chunk(i)],
            send_sem=send_done.at[i], recv_sem=recv_done.at[i],
            device_id=(r, c, mate), device_id_type=MESH,
        )

    def served(place, b):
        return place * parts + b != mate

    def to_serve(b):
        return seat * parts + b != f

    @pl.loop(0, CHUNKS)
    def _(i):
        @pl.when(sends_down(i))
        def _():
            along(f, i, False).start()

        @pl.when(sends_up(i))
        def _():
            along(f, i, True).start()

    for b in range(parts):
        for t in range(n_row // group):
            @pl.when(jnp.logical_not(mine & (owner == t)))
            def _():
                to_right(t, b).start()

    @pl.when(mine)
    def _():
        for b in range(parts):
            spot = right_at(right, c, seat, b)
            spot[...] = left[f, b * unit:(b + 1) * unit]

    def relay(d, i):
        @pl.when((f - d >= 0) & gets_up(i))
        def _():
            along(f - d, i, True).wait_recv()

            @pl.when(sends_up(i))
            def _():
                along(f - d, i, True).start()

        @pl.when((f + d < n_fib) & gets_down(i))
        def _():
            along(f + d, i, False).wait_recv()

            @pl.when(sends_down(i))
            def _():
                along(f + d, i, False).start()

    @pl.loop(0, CHUNKS)
    def _(i):
        relay(1, i)

    if helps:
        @pl.when(helper & mine)
        def _():
            for b in range(parts):
                @pl.when(served(seat, b))
                def _():
                    for t in range(n_row // group):
                        @pl.when(owner != t)
                        def _():
                            to_side(t, b).start()

                    spot = right_at(right_far, c, seat, b)
                    spot[...] = left[mate, b * unit:(b + 1) * unit]

    for b in range(parts):
        for col in range(n_col):
            @pl.when(jnp.logical_not(mine & (c == col)))
            def _():
                came_right(col, b).wait_recv()

            if helps:
                @pl.when(outer & (c != col) & to_serve(b))
                def _():
                    to_far(col, b).start()

            for other in range(group):
                @pl.when(seat != other)
                def _():
                    to_pair(col, b, other).start()

    for b in range(parts):
        for col in range(n_col):
            for other in range(group):
                @pl.when(seat != other)
                def _():
                    came_pair(col, b, other).wait_recv()

    near = jnp.where(has_down, f - 1, 1)
    first = jnp.where(has_down, f - 1, 0)
    ready = min(n_fib, 2)

    def product(ref, part, col, k):
        return jnp.dot(
            left[k, part, :],
            ref[
                pl.ds(pl.multiple_of(k * unit, unit), unit),
                pl.ds(pl.multiple_of(col * unit, unit), unit),
            ],
            preferred_element_type=jnp.float32,
        )

    def col_at(shift):
        return lax.rem(c + shift, n_col)

    def total_at(shift):
        return own if shift == 0 else ahead.at[shift - 1]

    wide = step * HELP

    @pl.loop(0, CHUNKS // HELP)
    def _(i):
        part = pl.ds(pl.multiple_of(i * wide, wide), wide)
        for shift in range(n_col):
            total_at(shift)[part, :] = product(right, part, col_at(shift), f)
        if ready > 1:
            @pl.when(jnp.logical_not(outer & (i * HELP < helps)))
            def _():
                for shift in range(n_col):
                    total_at(shift)[part, :] += product(right, part, col_at(shift), near)

    sums[r] = jnp.zeros((8, unit), jnp.float32)

    def combine(i, answered=False):
        part = chunk(i)
        expanded = own[part, :]
        for shift in range(1, n_col):
            came_col(col_at(shift), i).wait_recv()
            expanded += part_in[col_at(shift), part, :].astype(jnp.float32)
        if answered:
            to_done(i).wait_recv()
            expanded += helped[part, :].astype(jnp.float32)
        squared = expanded * expanded
        own[part, :] = squared
        sums[r] += jnp.sum(squared.reshape(step // 8, 8, unit), axis=0)

    def fetch():
        for b in range(parts):
            @pl.when(served(seat, b))
            def _():
                for col in range(n_col):
                    @pl.when(jnp.logical_not(mine & (c == col)))
                    def _():
                        came_far(col, b).wait_recv()

                    for other in range(group):
                        @pl.when(seat != other)
                        def _():
                            to_far_pair(col, b, other).start()

    def answer():
        for b in range(parts):
            for other in range(group):
                @pl.when((seat != other) & served(other, b))
                def _():
                    for col in range(n_col):
                        came_far_pair(col, b, other).wait_recv()

        part = pl.ds(0, helps * step)
        for shift in list(range(1, n_col)) + [0]:
            col = col_at(shift)
            total = product(right_far, part, col, lax.rem(mate + 1, n_fib))
            for k in range(2, n_fib):
                total += product(right_far, part, col, lax.rem(mate + k, n_fib))
            if shift:
                help_out[col, :, :] = total.astype(jnp.bfloat16)
                for i in range(helps):
                    to_help(col, i).start()
            else:
                help_own[...] = total

    @pl.loop(0, CHUNKS)
    def _(i):
        for d in range(2, n_fib):
            relay(d, i)

        if helps:
            @pl.when(helper & (i == FETCH))
            def _():
                fetch()

            @pl.when(helper & (i == ANSWER))
            def _():
                answer()

        part = chunk(i)
        full = jnp.logical_not(outer & (i < helps))

        @pl.when(full)
        def _():
            for shift in range(1, n_col):
                total = ahead[shift - 1, part, :]
                for k in range(ready, n_fib):
                    total += product(right, part, col_at(shift), lax.rem(first + k, n_fib))
                ahead[shift - 1, part, :] = total

        for shift in range(1, n_col):
            col = col_at(shift)
            part_out[col, part, :] = ahead[shift - 1, part, :].astype(jnp.bfloat16)
            to_col(col, i).start()

        @pl.when(full)
        def _():
            total = own[part, :]
            for k in range(ready, n_fib):
                total += product(right, part, c, lax.rem(first + k, n_fib))
            own[part, :] = total

        @pl.when((i >= LAG) & jnp.logical_not(outer & (i - LAG < helps)))
        def _():
            combine(i - LAG)

    @pl.loop(CHUNKS - LAG, CHUNKS - 1)
    def _(i):
        combine(i)

    if helps:
        @pl.when(helper)
        def _():
            @pl.loop(0, helps)
            def _(i):
                part = chunk(i)
                total = help_own[part, :]
                for shift in range(1, n_col):
                    came_help(col_at(shift), i).wait_recv()
                    total += help_in[col_at(shift), part, :].astype(jnp.float32)
                helped[part, :] = total.astype(jnp.bfloat16)
                to_done(i).start()

    combine(CHUNKS - 1)

    if helps:
        @pl.when(outer)
        def _():
            @pl.loop(0, helps)
            def _(i):
                combine(i, True)

    def to_row(shift):
        return pltpu.make_async_remote_copy(
            src_ref=sums.at[r], dst_ref=sums.at[r],
            send_sem=send_sum.at[shift], recv_sem=recv_sum.at[r],
            device_id=(lax.rem(r + shift, n_row), c, f), device_id_type=MESH,
        )

    def came_row(other):
        return pltpu.make_async_remote_copy(
            src_ref=sums.at[r], dst_ref=sums.at[other],
            send_sem=send_sum.at[0], recv_sem=recv_sum.at[other],
            device_id=(other, c, f), device_id_type=MESH,
        )

    for shift in range(1, n_row):
        to_row(shift).start()
    for shift in range(1, n_row):
        came_row(lax.rem(r + shift, n_row)).wait_recv()
    total = sums[0]
    for other in range(1, n_row):
        total += sums[other]
    scale = jnp.sum(total, axis=0, keepdims=True) / (rows * n_row) + 1e-6
    inverse_ref[...] = jnp.broadcast_to(1.0 / scale, inverse_ref.shape)

    @pl.loop(0, CHUNKS)
    def _(i):
        for source in range(n_fib):
            @pl.when(sends_up(i) & (source <= f))
            def _():
                along(source, i, True).wait_send()

            @pl.when(sends_down(i) & (source >= f))
            def _():
                along(source, i, False).wait_send()

        for shift in range(1, n_col):
            to_col(col_at(shift), i).wait_send()

    for b in range(parts):
        for t in range(n_row // group):
            @pl.when(jnp.logical_not(mine & (owner == t)))
            def _():
                to_right(t, b).wait_send()

        for col in range(n_col):
            for other in range(group):
                @pl.when(seat != other)
                def _():
                    to_pair(col, b, other).wait_send()

    if helps:
        @pl.when(helper)
        def _():
            for b in range(parts):
                @pl.when(served(seat, b))
                def _():
                    for t in range(n_row // group):
                        @pl.when(mine & (owner != t))
                        def _():
                            to_side(t, b).wait_send()

                    for col in range(n_col):
                        for other in range(group):
                            @pl.when(seat != other)
                            def _():
                                to_far_pair(col, b, other).wait_send()

            for i in range(helps):
                for shift in range(1, n_col):
                    to_help(col_at(shift), i).wait_send()
                to_done(i).wait_send()

        @pl.when(outer)
        def _():
            for b in range(parts):
                for col in range(n_col):
                    @pl.when((c != col) & to_serve(b))
                    def _():
                        to_far(col, b).wait_send()

    for shift in range(1, n_row):
        to_row(shift).wait_send()


def prune(keep_ref, squared_ref, inverse_ref, out_hbm, out_vmem, sem):
    tile = out_vmem.shape[1] // keep_ref.shape[0]
    copies = []
    for i in range(keep_ref.shape[1]):
        down = slice(i * tile, (i + 1) * tile)
        for j in range(keep_ref.shape[0]):
            across = slice(j * tile, (j + 1) * tile)
            factor = inverse_ref[0:1, across] * keep_ref[j, i].astype(jnp.float32)
            out_vmem[down, across] = squared_ref[down, across] * factor
        copy = pltpu.make_async_copy(out_vmem.at[down], out_hbm.at[down], sem.at[i])
        copy.start()
        copies.append(copy)
    for copy in copies:
        copy.wait()


def solution(mesh):
    n_row, n_col, n_fib = (mesh.shape[name] for name in ("row", "col", "fiber"))
    group = n_row // n_col
    helps = HELP if n_fib > 3 else 0

    def local(values, tile_mask, keep_mask):
        rows, unit = values.shape
        dma = pltpu.SemaphoreType.DMA
        parts = rows // unit
        few = rows // CHUNKS * HELP
        squared, inverse = pl.pallas_call(
            functools.partial(kernel, n_row, n_col, n_fib, helps),
            out_shape=(
                pltpu.VMEM((rows, unit), jnp.float32),
                pltpu.VMEM((8, unit), jnp.float32),
            ),
            in_specs=[
                pl.BlockSpec(memory_space=pltpu.HBM),
                pl.BlockSpec(memory_space=pltpu.HBM),
            ],
            out_specs=(
                pl.BlockSpec(memory_space=pltpu.VMEM),
                pl.BlockSpec(memory_space=pltpu.VMEM),
            ),
            scratch_shapes=[
                pltpu.SMEM(tile_mask.shape[::-1], jnp.int32),
                pltpu.VMEM((rows, unit), jnp.float32),
                pltpu.VMEM((n_fib, rows, unit), jnp.bfloat16),
                pltpu.VMEM((group * rows, n_col * unit), jnp.bfloat16),
                pltpu.VMEM((n_col - 1, rows, unit), jnp.float32),
                pltpu.VMEM((n_col, rows, unit), jnp.bfloat16),
                pltpu.VMEM((n_col, rows, unit), jnp.bfloat16),
                pltpu.VMEM((n_row, 8, unit), jnp.float32),
                pltpu.VMEM((group * rows, n_col * unit), jnp.bfloat16),
                pltpu.VMEM((few, unit), jnp.float32),
                pltpu.VMEM((n_col, few, unit), jnp.bfloat16),
                pltpu.VMEM((n_col, few, unit), jnp.bfloat16),
                pltpu.VMEM((few, unit), jnp.bfloat16),
                dma((2,)),
                dma((n_fib, CHUNKS)),
                dma((n_fib, CHUNKS)),
                dma((n_fib, CHUNKS)),
                dma((n_row // group, parts)),
                dma((n_col, parts)),
                dma((n_col, parts, group)),
                dma((n_col, parts, group)),
                dma((n_col, CHUNKS)),
                dma((n_col, CHUNKS)),
                dma((n_row,)),
                dma((n_row,)),
                dma((n_col, parts)),
                dma((n_row // group, parts)),
                dma((n_col, parts)),
                dma((n_col, parts, group)),
                dma((n_col, parts, group)),
                dma((n_col, HELP)),
                dma((n_col, HELP)),
                dma((HELP,)),
                dma((HELP,)),
            ],
            compiler_params=pltpu.CompilerParams(
                collective_id=0, has_side_effects=True, vmem_limit_bytes=VMEM_LIMIT
            ),
            name="expand",
        )(tile_mask.T, values)
        return pl.pallas_call(
            prune,
            out_shape=jax.ShapeDtypeStruct((rows, unit), jnp.float32),
            in_specs=[
                pl.BlockSpec(memory_space=pltpu.SMEM),
                pl.BlockSpec(memory_space=pltpu.VMEM),
                pl.BlockSpec(memory_space=pltpu.VMEM),
            ],
            out_specs=pl.BlockSpec(memory_space=pl.ANY),
            scratch_shapes=[
                pltpu.VMEM((rows, unit), jnp.float32),
                dma((keep_mask.shape[0],)),
            ],
            compiler_params=pltpu.CompilerParams(vmem_limit_bytes=8 * 1024 * 1024),
            name="prune",
        )(keep_mask.T, squared, inverse)

    spec = P("row", ("col", "fiber"))
    return jax.shard_map(
        local, mesh=mesh, in_specs=(spec, spec, spec), out_specs=spec, check_vma=False
    )
```

time: 53.2 us -> 52 us (0.977)
  Pallas kernels: 53 us -> 51.9 us
    pallas_call x1, Pallas kernels: 51.4 us -> 50.2 us  [local(): pl.pallas_call(functools.partial(kernel, n_row, n_col, n_fib, helps), out...]
where the time goes in v1:
time: 52 us; the launch traced here: 51.9 us
  Pallas kernels  51.9 us (100%)
    pallas_call x1, Pallas kernels, local(): pl.pallas_call(functools.partial(kernel, n_row, n_col, n_fib, helps), out...  50.2 us
    pallas_call x1, Pallas kernels, local(): pl.pallas_call(prune, out_shape=jax.ShapeDtypeStruct((rows, unit), jnp.fl...  1.64 us

profile of v1, /device:TPU:0, one launch (start us, length us, event | category | flops | bytes accessed | tf_op | source)
XLA Modules:
  0.0 51.9 jit_solution(7823408018114607335)
XLA Ops:
  0.0 0.0 copy-start
  0.0 50.2 %expand.1 = (f32[768,384]{1,0:T(8,128)S(1)}, f32[8,384]{1,0:T(8,128)S(1)}) custom-call(s32[3,6]{1,0:T(4,128)} %bitcast.3, f32[768,384]{1,0:T(8,128)} %values_hbm.1), custom_call_target="tpu_custom_call" | custom-call | tf_op jit(solution)/shard_map/expand/pallas_call | solution.py:537
  50.2 0.0 copy-done
  50.2 1.6 %prune.1 = f32[768,384]{1,0:T(8,128)} custom-call(s32[3,6]{1,0:T(4,128)S(1)} %bitcast.2, f32[768,384]{1,0:T(8,128)S(1)} %get-tuple-element.7.squared_ref, f32[8,384]{1,0:T(8,128)S(1)} %get-tuple-element.8.inverse_ref), custom_call_target="tpu_custom_call" | custom-call | tf_op jit(solution)/shard_map/prune/pallas_call | solution.py:592
Async XLA Ops:
  0.0 50.2 %copy-start = (s32[6,3]{0,1:T(4,128)S(1)}, s32[6,3]{0,1:T(4,128)}, u32[]{:S(2)}) copy-start(s32[6,3]{0,1:T(4,128)} %param.5) | copy-start | bytes 220

commit v2 on v1

--- a/solution.py
+++ b/solution.py
@@ -10,20 +10,20 @@
 MESH = pl.DeviceIdType.MESH
 CHUNKS = 8
 HELP = 2
-FETCH = 6
-ANSWER = 7
-LAG = 2
+AHEAD = 3
+FETCH = 4
+ANSWER = 5
+LAG = 3
 VMEM_LIMIT = 62 * 1024 * 1024
 
 
 def kernel(
     n_row, n_col, n_fib, helps, tile_hbm, values_hbm, own, inverse_ref,
-    tile_ref, values_ref, left, right, ahead, part_out, part_in, sums,
+    tile_ref, values_ref, left, right, part_out, part_in, sums,
     right_far, help_own, help_out, help_in, helped, load_sem,
-    send_up, send_down, recv_left, send_right, recv_right, send_pair, recv_pair,
-    send_part, recv_part, send_sum, recv_sum,
-    send_far, send_side, recv_far, send_far_pair, recv_far_pair,
-    send_help, recv_help, send_done, recv_done,
+    sent_left, sent_right, sent_pair, sent_part, sent_sum, sent_far, sent_far_pair, sent_help, sent_done,
+    recv_left, recv_right, recv_pair, recv_part, recv_sum,
+    recv_far, recv_far_pair, recv_help, recv_done,
 ):
     r, c, f = lax.axis_index("row"), lax.axis_index("col"), lax.axis_index("fiber")
     rows, unit = values_ref.shape
@@ -80,8 +80,7 @@
         part = left.at[source, chunk(i)]
         return pltpu.make_async_remote_copy(
             src_ref=part, dst_ref=part,
-            send_sem=(send_up if up else send_down).at[source, i],
-            recv_sem=recv_left.at[source, i],
+            send_sem=sent_left.at[int(up)], recv_sem=recv_left.at[source if up else source - 1, i],
             device_id=(r, c, f + 1 if up else f - 1), device_id_type=MESH,
         )
 
@@ -109,84 +108,87 @@
     def to_right(t, b):
         return pltpu.make_async_remote_copy(
             src_ref=block(f, b), dst_ref=right_at(right, c, seat, b),
-            send_sem=send_right.at[t, b], recv_sem=recv_right.at[c, b],
+            send_sem=sent_right.at[0], recv_sem=recv_right.at[c, b],
             device_id=(t * group + seat, owner, f), device_id_type=MESH,
         )
 
     def came_right(col, b):
         return pltpu.make_async_remote_copy(
             src_ref=block(f, b), dst_ref=right_at(right, col, seat, b),
-            send_sem=send_right.at[0, b], recv_sem=recv_right.at[col, b],
+            send_sem=sent_right.at[0], recv_sem=recv_right.at[col, b],
             device_id=(r, c, f), device_id_type=MESH,
         )
 
     def to_far(col, b):
         return pltpu.make_async_remote_copy(
             src_ref=right_at(right, col, seat, b), dst_ref=right_at(right_far, col, seat, b),
-            send_sem=send_far.at[col, b], recv_sem=recv_far.at[col, b],
+            send_sem=sent_far.at[0], recv_sem=recv_far.at[col, b],
             device_id=(r, c, mate), device_id_type=MESH,
         )
 
     def to_side(t, b):
         return pltpu.make_async_remote_copy(
             src_ref=block(mate, b), dst_ref=right_at(right_far, c, seat, b),
-            send_sem=send_side.at[t, b], recv_sem=recv_far.at[c, b],
+            send_sem=sent_far.at[0], recv_sem=recv_far.at[c, b],
             device_id=(t * group + seat, c, f), device_id_type=MESH,
         )
 
     def came_far(col, b):
         return pltpu.make_async_remote_copy(
             src_ref=block(f, b), dst_ref=right_at(right_far, col, seat, b),
-            send_sem=send_far.at[col, b], recv_sem=recv_far.at[col, b],
+            send_sem=sent_far.at[0], recv_sem=recv_far.at[col, b],
             device_id=(r, c, f), device_id_type=MESH,
         )
 
-    def pairing(ref, sends, recvs):
+    def pairing(ref, send, recv):
         def to_pair(col, b, other):
             return pltpu.make_async_remote_copy(
                 src_ref=right_at(ref, col, seat, b), dst_ref=right_at(ref, col, seat, b),
-                send_sem=sends.at[col, b, other], recv_sem=recvs.at[col, b, seat],
+                send_sem=send.at[0], recv_sem=recv.at[seat],
                 device_id=(owner * group + other, c, f), device_id_type=MESH,
             )
 
-        def came_pair(col, b, other):
+        def came_pair(other, blocks):
+            theirs = ref.at[pl.ds(other * rows, blocks * unit)]
             return pltpu.make_async_remote_copy(
-                src_ref=right_at(ref, col, other, b), dst_ref=right_at(ref, col, other, b),
-                send_sem=sends.at[col, b, other], recv_sem=recvs.at[col, b, other],
+                src_ref=theirs, dst_ref=theirs, send_sem=send.at[0], recv_sem=recv.at[other],
                 device_id=(r, c, f), device_id_type=MESH,
             )
 
         return to_pair, came_pair
 
-    to_pair, came_pair = pairing(right, send_pair, recv_pair)
-    to_far_pair, came_far_pair = pairing(right_far, send_far_pair, recv_far_pair)
-
-    def crossing(out, into, sends, recvs):
+    to_pair, came_pair = pairing(right, sent_pair, recv_pair)
+    to_far_pair, came_far_pair = pairing(right_far, sent_far_pair, recv_far_pair)
+
+    def crossing(out, into, send, recv):
         def to_col(col, i):
             return pltpu.make_async_remote_copy(
                 src_ref=out.at[col, chunk(i)], dst_ref=into.at[c, chunk(i)],
-                send_sem=sends.at[col, i], recv_sem=recvs.at[c, i],
+                send_sem=send.at[0], recv_sem=recv.at[lax.rem(c - col + n_col, n_col) - 1, i],
                 device_id=(r, col, f), device_id_type=MESH,
             )
 
         def came_col(col, i):
             return pltpu.make_async_remote_copy(
                 src_ref=out.at[col, chunk(i)], dst_ref=into.at[col, chunk(i)],
-                send_sem=sends.at[col, i], recv_sem=recvs.at[col, i],
+                send_sem=send.at[0], recv_sem=recv.at[lax.rem(col - c + n_col, n_col) - 1, i],
                 device_id=(r, col, f), device_id_type=MESH,
             )
 
         return to_col, came_col
 
-    to_col, came_col = crossing(part_out, part_in, send_part, recv_part)
-    to_help, came_help = crossing(help_out, help_in, send_help, recv_help)
+    to_col, came_col = crossing(part_out, part_in, sent_part, recv_part)
+    to_help, came_help = crossing(help_out, help_in, sent_help, recv_help)
 
     def to_done(i):
         return pltpu.make_async_remote_copy(
             src_ref=helped.at[chunk(i)], dst_ref=helped.at[chunk(i)],
-            send_sem=send_done.at[i], recv_sem=recv_done.at[i],
+            send_sem=sent_done.at[0], recv_sem=recv_done.at[i],
             device_id=(r, c, mate), device_id_type=MESH,
         )
+
+    def skips(place, far):
+        return (far >= place * parts) & (far < (place + 1) * parts)
 
     def served(place, b):
         return place * parts + b != mate
@@ -194,15 +196,23 @@
     def to_serve(b):
         return seat * parts + b != f
 
+    def send_own(i, now_down, now_up):
+        @pl.when(sends_down(i) & now_down)
+        def _():
+            along(f, i, False).start()
+
+        @pl.when(sends_up(i) & now_up)
+        def _():
+            along(f, i, True).start()
+
+    last = max(n_fib - 3, 0) * AHEAD
+    before = last + 2
+    direct_down = outer | (f == 1)
+    direct_up = outer | (f == n_fib - 2)
+
     @pl.loop(0, CHUNKS)
     def _(i):
-        @pl.when(sends_down(i))
-        def _():
-            along(f, i, False).start()
-
-        @pl.when(sends_up(i))
-        def _():
-            along(f, i, True).start()
+        send_own(i, direct_down | (i < AHEAD), direct_up | (i < AHEAD))
 
     for b in range(parts):
         for t in range(n_row // group):
@@ -216,7 +226,7 @@
             spot = right_at(right, c, seat, b)
             spot[...] = left[f, b * unit:(b + 1) * unit]
 
-    def relay(d, i):
+    def pass_up(d, i):
         @pl.when((f - d >= 0) & gets_up(i))
         def _():
             along(f - d, i, True).wait_recv()
@@ -225,6 +235,7 @@
             def _():
                 along(f - d, i, True).start()
 
+    def pass_down(d, i):
         @pl.when((f + d < n_fib) & gets_down(i))
         def _():
             along(f + d, i, False).wait_recv()
@@ -233,23 +244,63 @@
             def _():
                 along(f + d, i, False).start()
 
-    @pl.loop(0, CHUNKS)
-    def _(i):
-        relay(1, i)
-
-    if helps:
-        @pl.when(helper & mine)
-        def _():
-            for b in range(parts):
-                @pl.when(served(seat, b))
+    def relay(s):
+        @pl.when(s < CHUNKS - AHEAD)
+        def _():
+            send_own(s + AHEAD, jnp.logical_not(direct_down), jnp.logical_not(direct_up))
+
+        @pl.when((s < CHUNKS) & ((s < before) | (f != 1)))
+        def _():
+            pass_up(1, s)
+
+        @pl.when((s < CHUNKS) & ((s < before) | (f != n_fib - 2)))
+        def _():
+            pass_down(1, s)
+
+        for d in range(2, n_fib - 1):
+            i = s - (d - 1) * AHEAD
+
+            @pl.when((i >= 0) & (i < CHUNKS))
+            def _():
+                pass_up(d, i)
+                pass_down(d, i)
+
+    def side(b):
+        @pl.when(helper & mine & served(seat, b))
+        def _():
+            for t in range(n_row // group):
+                @pl.when(owner != t)
                 def _():
-                    for t in range(n_row // group):
-                        @pl.when(owner != t)
-                        def _():
-                            to_side(t, b).start()
-
-                    spot = right_at(right_far, c, seat, b)
-                    spot[...] = left[mate, b * unit:(b + 1) * unit]
+                    to_side(t, b).start()
+
+            spot = right_at(right_far, c, seat, b)
+            spot[...] = left[mate, b * unit:(b + 1) * unit]
+
+    early = [b for b in range(parts) if (b + 1) * unit <= before * step]
+
+    @pl.when(jnp.logical_not(outer))
+    def _():
+        @pl.loop(0, before)
+        def _(s):
+            relay(s)
+
+        if helps:
+            for b in early:
+                side(b)
+
+        @pl.loop(before, CHUNKS)
+        def _(i):
+            @pl.when(f == 1)
+            def _():
+                pass_up(1, i)
+
+            @pl.when(f == n_fib - 2)
+            def _():
+                pass_down(1, i)
+
+        if helps:
+            for b in range(len(early), parts):
+                side(b)
 
     for b in range(parts):
         for col in range(n_col):
@@ -267,16 +318,10 @@
                 def _():
                     to_pair(col, b, other).start()
 
-    for b in range(parts):
-        for col in range(n_col):
-            for other in range(group):
-                @pl.when(seat != other)
-                def _():
-                    came_pair(col, b, other).wait_recv()
-
-    near = jnp.where(has_down, f - 1, 1)
-    first = jnp.where(has_down, f - 1, 0)
-    ready = min(n_fib, 2)
+    for other in range(group):
+        @pl.when(seat != other)
+        def _():
+            came_pair(other, parts).wait_recv()
 
     def product(ref, part, col, k):
         return jnp.dot(
@@ -288,24 +333,14 @@
             preferred_element_type=jnp.float32,
         )
 
+    def all_products(part, col):
+        total = product(right, part, col, 0)
+        for k in range(1, n_fib):
+            total += product(right, part, col, k)
+        return total
+
     def col_at(shift):
         return lax.rem(c + shift, n_col)
-
-    def total_at(shift):
-        return own if shift == 0 else ahead.at[shift - 1]
-
-    wide = step * HELP
-
-    @pl.loop(0, CHUNKS // HELP)
-    def _(i):
-        part = pl.ds(pl.multiple_of(i * wide, wide), wide)
-        for shift in range(n_col):
-            total_at(shift)[part, :] = product(right, part, col_at(shift), f)
-        if ready > 1:
-            @pl.when(jnp.logical_not(outer & (i * HELP < helps)))
-            def _():
-                for shift in range(n_col):
-                    total_at(shift)[part, :] += product(right, part, col_at(shift), near)
 
     sums[r] = jnp.zeros((8, unit), jnp.float32)
 
@@ -337,12 +372,11 @@
                             to_far_pair(col, b, other).start()
 
     def answer():
-        for b in range(parts):
-            for other in range(group):
-                @pl.when((seat != other) & served(other, b))
+        for other in range(group):
+            for skipped in range(2):
+                @pl.when((seat != other) & (skips(other, mate) == bool(skipped)))
                 def _():
-                    for col in range(n_col):
-                        came_far_pair(col, b, other).wait_recv()
+                    came_far_pair(other, parts - skipped).wait_recv()
 
         part = pl.ds(0, helps * step)
         for shift in list(range(1, n_col)) + [0]:
@@ -359,8 +393,14 @@
 
     @pl.loop(0, CHUNKS)
     def _(i):
-        for d in range(2, n_fib):
-            relay(d, i)
+        part = chunk(i)
+        full = jnp.logical_not(outer & (i < helps))
+
+        @pl.when(outer & full)
+        def _():
+            for d in range(1, n_fib):
+                pass_up(d, i)
+                pass_down(d, i)
 
         if helps:
             @pl.when(helper & (i == FETCH))
@@ -371,28 +411,32 @@
             def _():
                 answer()
 
-        part = chunk(i)
-        full = jnp.logical_not(outer & (i < helps))
-
         @pl.when(full)
         def _():
             for shift in range(1, n_col):
-                total = ahead[shift - 1, part, :]
-                for k in range(ready, n_fib):
-                    total += product(right, part, col_at(shift), lax.rem(first + k, n_fib))
-                ahead[shift - 1, part, :] = total
+                col = col_at(shift)
+                part_out[col, part, :] = all_products(part, col).astype(jnp.bfloat16)
+
+        @pl.when(jnp.logical_not(full))
+        def _():
+            for shift in range(1, n_col):
+                col = col_at(shift)
+                part_out[col, part, :] = product(right, part, col, f).astype(jnp.bfloat16)
 
         for shift in range(1, n_col):
-            col = col_at(shift)
-            part_out[col, part, :] = ahead[shift - 1, part, :].astype(jnp.bfloat16)
-            to_col(col, i).start()
+            to_col(col_at(shift), i).start()
 
         @pl.when(full)
         def _():
-            total = own[part, :]
-            for k in range(ready, n_fib):
-                total += product(right, part, c, lax.rem(first + k, n_fib))
-            own[part, :] = total
+            own[part, :] = all_products(part, c)
+
+        @pl.when(jnp.logical_not(full))
+        def _():
+            own[part, :] = product(right, part, c, f)
+
+        @pl.when(jnp.logical_not(outer) & (i + before < CHUNKS + last))
+        def _():
+            relay(i + before)
 
         @pl.when((i >= LAG) & jnp.logical_not(outer & (i - LAG < helps)))
         def _():
@@ -427,85 +471,77 @@
     def to_row(shift):
         return pltpu.make_async_remote_copy(
             src_ref=sums.at[r], dst_ref=sums.at[r],
-            send_sem=send_sum.at[shift], recv_sem=recv_sum.at[r],
+            send_sem=sent_sum.at[0], recv_sem=recv_sum.at[0],
             device_id=(lax.rem(r + shift, n_row), c, f), device_id_type=MESH,
         )
 
-    def came_row(other):
-        return pltpu.make_async_remote_copy(
-            src_ref=sums.at[r], dst_ref=sums.at[other],
-            send_sem=send_sum.at[0], recv_sem=recv_sum.at[other],
-            device_id=(other, c, f), device_id_type=MESH,
+    def came_rows():
+        return pltpu.make_async_remote_copy(
+            src_ref=sums.at[pl.ds(0, n_row - 1)], dst_ref=sums.at[pl.ds(0, n_row - 1)],
+            send_sem=sent_sum.at[0], recv_sem=recv_sum.at[0],
+            device_id=(r, c, f), device_id_type=MESH,
         )
 
     for shift in range(1, n_row):
         to_row(shift).start()
-    for shift in range(1, n_row):
-        came_row(lax.rem(r + shift, n_row)).wait_recv()
+    came_rows().wait_recv()
     total = sums[0]
     for other in range(1, n_row):
         total += sums[other]
     scale = jnp.sum(total, axis=0, keepdims=True) / (rows * n_row) + 1e-6
     inverse_ref[...] = jnp.broadcast_to(1.0 / scale, inverse_ref.shape)
 
-    @pl.loop(0, CHUNKS)
-    def _(i):
-        for source in range(n_fib):
-            @pl.when(sends_up(i) & (source <= f))
-            def _():
-                along(source, i, True).wait_send()
-
-            @pl.when(sends_down(i) & (source >= f))
-            def _():
-                along(source, i, False).wait_send()
-
-        for shift in range(1, n_col):
-            to_col(col_at(shift), i).wait_send()
-
-    for b in range(parts):
-        for t in range(n_row // group):
-            @pl.when(jnp.logical_not(mine & (owner == t)))
-            def _():
-                to_right(t, b).wait_send()
-
-        for col in range(n_col):
-            for other in range(group):
-                @pl.when(seat != other)
+    def left_behind(sem, ref):
+        pltpu.make_async_remote_copy(
+            src_ref=ref, dst_ref=ref, send_sem=sem, recv_sem=recv_sum.at[0],
+            device_id=(r, c, f), device_id_type=MESH,
+        ).wait_send()
+
+    few = helps * step
+    for at in range(n_fib):
+        @pl.when(f == at)
+        def _():
+            if at < n_fib - 1:
+                less = few if at == n_fib - 2 else 0
+                left_behind(sent_left.at[1], left.at[pl.ds(0, at + 1), pl.ds(0, rows - less)])
+            if at > 0:
+                less = few if at == 1 else 0
+                left_behind(sent_left.at[0], left.at[pl.ds(0, n_fib - at), pl.ds(0, rows - less)])
+
+    for less in range(2):
+        if n_col > less:
+            @pl.when(mine == bool(less))
+            def _():
+                left_behind(sent_right.at[0], part_out.at[pl.ds(0, n_col - less)])
+
+    if group > 1:
+        left_behind(sent_pair.at[0], right.at[pl.ds(0, (group - 1) * rows)])
+    if n_col > 1:
+        left_behind(sent_part.at[0], part_out.at[pl.ds(0, n_col - 1)])
+    if n_row > 1:
+        left_behind(sent_sum.at[0], sums.at[pl.ds(0, n_row - 1)])
+
+    if helps:
+        for less in range(2):
+            size = (parts - less) * unit
+            across = pl.ds(0, (n_col - 1) * unit)
+            if size and n_col > 1:
+                @pl.when(skips(seat, jnp.where(outer, f, mate)) == bool(less))
                 def _():
-                    to_pair(col, b, other).wait_send()
-
-    if helps:
+                    @pl.when(outer | (helper & mine))
+                    def _():
+                        left_behind(sent_far.at[0], right.at[pl.ds(0, size), across])
+
+            if size and group > 1:
+                @pl.when(helper & (skips(seat, mate) == bool(less)))
+                def _():
+                    left_behind(sent_far_pair.at[0], right.at[pl.ds(0, (group - 1) * size)])
+
         @pl.when(helper)
         def _():
-            for b in range(parts):
-                @pl.when(served(seat, b))
-                def _():
-                    for t in range(n_row // group):
-                        @pl.when(mine & (owner != t))
-                        def _():
-                            to_side(t, b).wait_send()
-
-                    for col in range(n_col):
-                        for other in range(group):
-                            @pl.when(seat != other)
-                            def _():
-                                to_far_pair(col, b, other).wait_send()
-
-            for i in range(helps):
-                for shift in range(1, n_col):
-                    to_help(col_at(shift), i).wait_send()
-                to_done(i).wait_send()
-
-        @pl.when(outer)
-        def _():
-            for b in range(parts):
-                for col in range(n_col):
-                    @pl.when((c != col) & to_serve(b))
-                    def _():
-                        to_far(col, b).wait_send()
-
-    for shift in range(1, n_row):
-        to_row(shift).wait_send()
+            if n_col > 1:
+                left_behind(sent_help.at[0], help_out.at[pl.ds(0, n_col - 1)])
+            left_behind(sent_done.at[0], helped)
 
 
 def prune(keep_ref, squared_ref, inverse_ref, out_hbm, out_vmem, sem):
@@ -553,7 +589,6 @@
                 pltpu.VMEM((rows, unit), jnp.float32),
                 pltpu.VMEM((n_fib, rows, unit), jnp.bfloat16),
                 pltpu.VMEM((group * rows, n_col * unit), jnp.bfloat16),
-                pltpu.VMEM((n_col - 1, rows, unit), jnp.float32),
                 pltpu.VMEM((n_col, rows, unit), jnp.bfloat16),
                 pltpu.VMEM((n_col, rows, unit), jnp.bfloat16),
                 pltpu.VMEM((n_row, 8, unit), jnp.float32),
@@ -563,25 +598,23 @@
                 pltpu.VMEM((n_col, few, unit), jnp.bfloat16),
                 pltpu.VMEM((few, unit), jnp.bfloat16),
                 dma((2,)),
-                dma((n_fib, CHUNKS)),
-                dma((n_fib, CHUNKS)),
-                dma((n_fib, CHUNKS)),
-                dma((n_row // group, parts)),
+                dma((2,)),
+                dma((1,)),
+                dma((1,)),
+                dma((1,)),
+                dma((1,)),
+                dma((1,)),
+                dma((1,)),
+                dma((1,)),
+                dma((1,)),
+                dma((n_fib - 1, CHUNKS)),
                 dma((n_col, parts)),
-                dma((n_col, parts, group)),
-                dma((n_col, parts, group)),
-                dma((n_col, CHUNKS)),
-                dma((n_col, CHUNKS)),
-                dma((n_row,)),
-                dma((n_row,)),
+                dma((group,)),
+                dma((n_col - 1, CHUNKS)),
+                dma((1,)),
                 dma((n_col, parts)),
-                dma((n_row // group, parts)),
-                dma((n_col, parts)),
-                dma((n_col, parts, group)),
-                dma((n_col, parts, group)),
-                dma((n_col, HELP)),
-                dma((n_col, HELP)),
-                dma((HELP,)),
+                dma((group,)),
+                dma((n_col - 1, HELP)),
                 dma((HELP,)),
             ],
             compiler_params=pltpu.CompilerParams(

time: 52 us -> 50.9 us (0.979)
  Pallas kernels: 51.9 us -> 50.7 us
    pallas_call x1, Pallas kernels: 50.2 us -> 49.1 us  [local(): pl.pallas_call(functools.partial(kernel, n_row, n_col, n_fib, helps), out...]
where the time goes in v2:
time: 50.9 us; the launch traced here: 50.8 us
  Pallas kernels  50.7 us (100%)
    pallas_call x1, Pallas kernels, local(): pl.pallas_call(functools.partial(kernel, n_row, n_col, n_fib, helps), out...  49.1 us
    pallas_call x1, Pallas kernels, local(): pl.pallas_call(prune, out_shape=jax.ShapeDtypeStruct((rows, unit), jnp.fl...  1.64 us

profile of v2, /device:TPU:0, one launch (start us, length us, event | category | flops | bytes accessed | tf_op | source)
XLA Modules:
  0.0 50.8 jit_solution(10687620392149107984)
XLA Ops:
  0.0 0.0 copy-start
  0.0 49.1 %expand.1 = (f32[768,384]{1,0:T(8,128)S(1)}, f32[8,384]{1,0:T(8,128)S(1)}) custom-call(s32[3,6]{1,0:T(4,128)} %bitcast.3, f32[768,384]{1,0:T(8,128)} %values_hbm.1), custom_call_target="tpu_custom_call" | custom-call | tf_op jit(solution)/shard_map/expand/pallas_call | solution.py:573
  49.1 0.0 copy-done
  49.1 1.6 %prune.1 = f32[768,384]{1,0:T(8,128)} custom-call(s32[3,6]{1,0:T(4,128)S(1)} %bitcast.2, f32[768,384]{1,0:T(8,128)S(1)} %get-tuple-element.7.squared_ref, f32[8,384]{1,0:T(8,128)S(1)} %get-tuple-element.8.inverse_ref), custom_call_target="tpu_custom_call" | custom-call | tf_op jit(solution)/shard_map/prune/pallas_call | solution.py:625
Async XLA Ops:
  0.0 49.1 %copy-start = (s32[6,3]{0,1:T(4,128)S(1)}, s32[6,3]{0,1:T(4,128)}, u32[]{:S(2)}) copy-start(s32[6,3]{0,1:T(4,128)} %param.5) | copy-start | bytes 220

commit v3 on v2

--- a/solution.py
+++ b/solution.py
@@ -8,12 +8,13 @@
 from jax.sharding import PartitionSpec as P
 
 MESH = pl.DeviceIdType.MESH
-CHUNKS = 8
-HELP = 2
-AHEAD = 3
-FETCH = 4
-ANSWER = 5
-LAG = 3
+CHUNKS = 12
+HELP = 3
+TRAIL = 1
+AHEAD = 5
+FETCH = 7
+ANSWER = 8
+LAG = 4
 VMEM_LIMIT = 62 * 1024 * 1024
 
 
@@ -74,7 +75,7 @@
     pl.semaphore_wait(barrier, n_row * n_col - 1 + neighbours)
 
     def chunk(i):
-        return pl.ds(pl.multiple_of(i * step, step), step)
+        return pl.ds(i * step if isinstance(i, int) else pl.multiple_of(i * step, step), step)
 
     def along(source, i, up):
         part = left.at[source, chunk(i)]
@@ -84,17 +85,25 @@
             device_id=(r, c, f + 1 if up else f - 1), device_id_type=MESH,
         )
 
+    lead, trail = helps - min(helps, TRAIL), CHUNKS - min(helps, TRAIL)
+
+    def kept(i):
+        return (i >= lead) & (i < trail)
+
+    def lent_at(h):
+        return h if h < lead else h - helps + CHUNKS
+
     def sends_up(i):
-        return has_up & ((i >= helps) | (f + 1 < n_fib - 1))
+        return has_up & (kept(i) | (f + 1 < n_fib - 1))
 
     def sends_down(i):
-        return has_down & ((i >= helps) | (f - 1 > 0))
+        return has_down & (kept(i) | (f - 1 > 0))
 
     def gets_up(i):
-        return (i >= helps) | has_up
+        return kept(i) | has_up
 
     def gets_down(i):
-        return (i >= helps) | has_down
+        return kept(i) | has_down
 
     def right_at(ref, col, place, b):
         return ref.at[
@@ -245,9 +254,11 @@
                 along(f + d, i, False).start()
 
     def relay(s):
-        @pl.when(s < CHUNKS - AHEAD)
+        @pl.when(jnp.asarray(s) < CHUNKS - AHEAD)
         def _():
             send_own(s + AHEAD, jnp.logical_not(direct_down), jnp.logical_not(direct_up))
+
+        s = jnp.asarray(s)
 
         @pl.when((s < CHUNKS) & ((s < before) | (f != 1)))
         def _():
@@ -276,33 +287,7 @@
             spot = right_at(right_far, c, seat, b)
             spot[...] = left[mate, b * unit:(b + 1) * unit]
 
-    early = [b for b in range(parts) if (b + 1) * unit <= before * step]
-
-    @pl.when(jnp.logical_not(outer))
-    def _():
-        @pl.loop(0, before)
-        def _(s):
-            relay(s)
-
-        if helps:
-            for b in early:
-                side(b)
-
-        @pl.loop(before, CHUNKS)
-        def _(i):
-            @pl.when(f == 1)
-            def _():
-                pass_up(1, i)
-
-            @pl.when(f == n_fib - 2)
-            def _():
-                pass_down(1, i)
-
-        if helps:
-            for b in range(len(early), parts):
-                side(b)
-
-    for b in range(parts):
+    def gather(b):
         for col in range(n_col):
             @pl.when(jnp.logical_not(mine & (c == col)))
             def _():
@@ -317,6 +302,41 @@
                 @pl.when(seat != other)
                 def _():
                     to_pair(col, b, other).start()
+
+    early = [b for b in range(parts) if (b + 1) * unit <= before * step]
+
+    @pl.when(jnp.logical_not(outer))
+    def _():
+        @pl.loop(0, before - 1)
+        def _(s):
+            relay(s)
+
+    for b in range(parts - 1):
+        gather(b)
+
+    @pl.when(jnp.logical_not(outer))
+    def _():
+        relay(before - 1)
+
+        if helps:
+            for b in early:
+                side(b)
+
+        @pl.loop(before, CHUNKS)
+        def _(i):
+            @pl.when(f == 1)
+            def _():
+                pass_up(1, i)
+
+            @pl.when(f == n_fib - 2)
+            def _():
+                pass_down(1, i)
+
+        if helps:
+            for b in range(len(early), parts):
+                side(b)
+
+    gather(parts - 1)
 
     for other in range(group):
         @pl.when(seat != other)
@@ -344,15 +364,15 @@
 
     sums[r] = jnp.zeros((8, unit), jnp.float32)
 
-    def combine(i, answered=False):
+    def combine(i, h=None):
         part = chunk(i)
         expanded = own[part, :]
         for shift in range(1, n_col):
             came_col(col_at(shift), i).wait_recv()
             expanded += part_in[col_at(shift), part, :].astype(jnp.float32)
-        if answered:
-            to_done(i).wait_recv()
-            expanded += helped[part, :].astype(jnp.float32)
+        if h is not None:
+            to_done(h).wait_recv()
+            expanded += helped[pl.ds(h * step, step), :].astype(jnp.float32)
         squared = expanded * expanded
         own[part, :] = squared
         sums[r] += jnp.sum(squared.reshape(step // 8, 8, unit), axis=0)
@@ -378,23 +398,41 @@
                 def _():
                     came_far_pair(other, parts - skipped).wait_recv()
 
-        part = pl.ds(0, helps * step)
+        reckon(0, lead)
+
+    def reckon(h, count):
+        if count == 0:
+            return
+        part = pl.ds(lent_at(h) * step, count * step)
+        there = pl.ds(h * step, count * step)
         for shift in list(range(1, n_col)) + [0]:
             col = col_at(shift)
             total = product(right_far, part, col, lax.rem(mate + 1, n_fib))
             for k in range(2, n_fib):
                 total += product(right_far, part, col, lax.rem(mate + k, n_fib))
             if shift:
-                help_out[col, :, :] = total.astype(jnp.bfloat16)
-                for i in range(helps):
+                help_out[col, there, :] = total.astype(jnp.bfloat16)
+                for i in range(h, h + count):
                     to_help(col, i).start()
             else:
-                help_own[...] = total
+                help_own[there, :] = total
+
+    if helps:
+        @pl.when(outer)
+        def _():
+            for h in range(helps):
+                i = lent_at(h)
+                part = pl.ds(i * step, step)
+                for shift in range(1, n_col):
+                    col = col_at(shift)
+                    part_out[col, part, :] = product(right, part, col, f).astype(jnp.bfloat16)
+                    to_col(col, i).start()
+                own[part, :] = product(right, part, c, f)
 
     @pl.loop(0, CHUNKS)
     def _(i):
         part = chunk(i)
-        full = jnp.logical_not(outer & (i < helps))
+        full = kept(i) | jnp.logical_not(outer)
 
         @pl.when(outer & full)
         def _():
@@ -411,62 +449,56 @@
             def _():
                 answer()
 
+            for h in range(lead, helps):
+                @pl.when(helper & (i == lent_at(h)))
+                def _():
+                    reckon(h, 1)
+
         @pl.when(full)
         def _():
             for shift in range(1, n_col):
                 col = col_at(shift)
                 part_out[col, part, :] = all_products(part, col).astype(jnp.bfloat16)
-
-        @pl.when(jnp.logical_not(full))
-        def _():
+                to_col(col, i).start()
+
+            own[part, :] = all_products(part, c)
+
+        @pl.when(jnp.logical_not(outer) & (i + before < CHUNKS + last))
+        def _():
+            relay(i + before)
+
+        @pl.when((i >= LAG) & (kept(i - LAG) | jnp.logical_not(outer)))
+        def _():
+            combine(i - LAG)
+
+    def reply(h):
+        @pl.when(helper)
+        def _():
+            part = pl.ds(h * step, step)
+            total = help_own[part, :]
             for shift in range(1, n_col):
-                col = col_at(shift)
-                part_out[col, part, :] = product(right, part, col, f).astype(jnp.bfloat16)
-
-        for shift in range(1, n_col):
-            to_col(col_at(shift), i).start()
-
-        @pl.when(full)
-        def _():
-            own[part, :] = all_products(part, c)
-
-        @pl.when(jnp.logical_not(full))
-        def _():
-            own[part, :] = product(right, part, c, f)
-
-        @pl.when(jnp.logical_not(outer) & (i + before < CHUNKS + last))
-        def _():
-            relay(i + before)
-
-        @pl.when((i >= LAG) & jnp.logical_not(outer & (i - LAG < helps)))
-        def _():
-            combine(i - LAG)
-
-    @pl.loop(CHUNKS - LAG, CHUNKS - 1)
-    def _(i):
-        combine(i)
-
-    if helps:
-        @pl.when(helper)
-        def _():
-            @pl.loop(0, helps)
-            def _(i):
-                part = chunk(i)
-                total = help_own[part, :]
-                for shift in range(1, n_col):
-                    came_help(col_at(shift), i).wait_recv()
-                    total += help_in[col_at(shift), part, :].astype(jnp.float32)
-                helped[part, :] = total.astype(jnp.bfloat16)
-                to_done(i).start()
-
-    combine(CHUNKS - 1)
+                came_help(col_at(shift), h).wait_recv()
+                total += help_in[col_at(shift), part, :].astype(jnp.float32)
+            helped[part, :] = total.astype(jnp.bfloat16)
+            to_done(h).start()
+
+    for h in range(lead):
+        reply(h)
+
+    for i in range(CHUNKS - LAG, CHUNKS):
+        for h in range(lead, helps):
+            if lent_at(h) == i:
+                reply(h)
+
+        @pl.when(kept(jnp.asarray(i)) | jnp.logical_not(outer))
+        def _():
+            combine(i)
 
     if helps:
         @pl.when(outer)
         def _():
-            @pl.loop(0, helps)
-            def _(i):
-                combine(i, True)
+            for h in range(helps):
+                combine(lent_at(h), h)
 
     def to_row(shift):
         return pltpu.make_async_remote_copy(

time: 50.9 us -> 48.8 us (0.959)
  Pallas kernels: 50.7 us -> 48.6 us
    pallas_call x1, Pallas kernels: 49.1 us -> 47 us  [local(): pl.pallas_call(functools.partial(kernel, n_row, n_col, n_fib, helps), out...]
where the time goes in v3:
time: 48.8 us; the launch traced here: 48.7 us
  Pallas kernels  48.6 us (100%)
    pallas_call x1, Pallas kernels, local(): pl.pallas_call(functools.partial(kernel, n_row, n_col, n_fib, helps), out...  47 us
    pallas_call x1, Pallas kernels, local(): pl.pallas_call(prune, out_shape=jax.ShapeDtypeStruct((rows, unit), jnp.fl...  1.64 us

profile of v3, /device:TPU:0, one launch (start us, length us, event | category | flops | bytes accessed | tf_op | source)
XLA Modules:
  0.0 48.7 jit_solution(5312302167276070039)
XLA Ops:
  0.0 0.0 copy-start
  0.0 47.0 %expand.1 = (f32[768,384]{1,0:T(8,128)S(1)}, f32[8,384]{1,0:T(8,128)S(1)}) custom-call(s32[3,6]{1,0:T(4,128)} %bitcast.3, f32[768,384]{1,0:T(8,128)} %values_hbm.1), custom_call_target="tpu_custom_call" | custom-call | tf_op jit(solution)/shard_map/expand/pallas_call | solution.py:605
  47.0 0.0 copy-done
  47.0 1.6 %prune.1 = f32[768,384]{1,0:T(8,128)} custom-call(s32[3,6]{1,0:T(4,128)S(1)} %bitcast.2, f32[768,384]{1,0:T(8,128)S(1)} %get-tuple-element.7.squared_ref, f32[8,384]{1,0:T(8,128)S(1)} %get-tuple-element.8.inverse_ref), custom_call_target="tpu_custom_call" | custom-call | tf_op jit(solution)/shard_map/prune/pallas_call | solution.py:657
Async XLA Ops:
  0.0 47.0 %copy-start = (s32[6,3]{0,1:T(4,128)S(1)}, s32[6,3]{0,1:T(4,128)}, u32[]{:S(2)}) copy-start(s32[6,3]{0,1:T(4,128)} %param.5) | copy-start | bytes 220

commit v4 on v3

--- a/solution.py
+++ b/solution.py
@@ -10,10 +10,9 @@
 MESH = pl.DeviceIdType.MESH
 CHUNKS = 12
 HELP = 3
-TRAIL = 1
-AHEAD = 5
-FETCH = 7
-ANSWER = 8
+AHEAD = 3
+FETCH = 8
+ANSWER = 9
 LAG = 4
 VMEM_LIMIT = 62 * 1024 * 1024
 
@@ -85,13 +84,8 @@
             device_id=(r, c, f + 1 if up else f - 1), device_id_type=MESH,
         )
 
-    lead, trail = helps - min(helps, TRAIL), CHUNKS - min(helps, TRAIL)
-
     def kept(i):
-        return (i >= lead) & (i < trail)
-
-    def lent_at(h):
-        return h if h < lead else h - helps + CHUNKS
+        return i >= helps
 
     def sends_up(i):
         return has_up & (kept(i) | (f + 1 < n_fib - 1))
@@ -214,10 +208,10 @@
         def _():
             along(f, i, True).start()
 
-    last = max(n_fib - 3, 0) * AHEAD
-    before = last + 2
-    direct_down = outer | (f == 1)
-    direct_up = outer | (f == n_fib - 2)
+    low, high = f == 1, f == n_fib - 2
+    inner = jnp.logical_not(outer)
+    direct_down = outer | jnp.logical_not(high)
+    direct_up = outer | jnp.logical_not(low)
 
     @pl.loop(0, CHUNKS)
     def _(i):
@@ -253,28 +247,32 @@
             def _():
                 along(f + d, i, False).start()
 
-    def relay(s):
-        @pl.when(jnp.asarray(s) < CHUNKS - AHEAD)
-        def _():
-            send_own(s + AHEAD, jnp.logical_not(direct_down), jnp.logical_not(direct_up))
-
-        s = jnp.asarray(s)
-
-        @pl.when((s < CHUNKS) & ((s < before) | (f != 1)))
-        def _():
-            pass_up(1, s)
-
-        @pl.when((s < CHUNKS) & ((s < before) | (f != n_fib - 2)))
-        def _():
-            pass_down(1, s)
-
+    def feed(i):
+        @pl.when(low)
+        def _():
+            pass_up(1, i)
+
+        @pl.when(high)
+        def _():
+            pass_down(1, i)
+
+        @pl.when(i + AHEAD < CHUNKS)
+        def _():
+            send_own(i + AHEAD, high, low)
+
+    def near(i):
+        @pl.when(jnp.logical_not(low))
+        def _():
+            pass_up(1, i)
+
+        @pl.when(jnp.logical_not(high))
+        def _():
+            pass_down(1, i)
+
+    def far(i):
         for d in range(2, n_fib - 1):
-            i = s - (d - 1) * AHEAD
-
-            @pl.when((i >= 0) & (i < CHUNKS))
-            def _():
-                pass_up(d, i)
-                pass_down(d, i)
+            pass_up(d, i)
+            pass_down(d, i)
 
     def side(b):
         @pl.when(helper & mine & served(seat, b))
@@ -303,38 +301,31 @@
                 def _():
                     to_pair(col, b, other).start()
 
-    early = [b for b in range(parts) if (b + 1) * unit <= before * step]
-
-    @pl.when(jnp.logical_not(outer))
+    half = CHUNKS // 2
+
+    def approach(first, last):
+        @pl.when(inner)
+        def _():
+            @pl.loop(first, last)
+            def _(p):
+                feed(2 * p)
+                near(p)
+                feed(2 * p + 1)
+
+                @pl.when(p > 1)
+                def _():
+                    far(p - 2)
+
+    for b in range(parts):
+        approach(half * b // parts, half * (b + 1) // parts)
+        if helps:
+            side(b)
+        if b < parts - 1:
+            gather(b)
+
+    @pl.when(inner)
     def _():
-        @pl.loop(0, before - 1)
-        def _(s):
-            relay(s)
-
-    for b in range(parts - 1):
-        gather(b)
-
-    @pl.when(jnp.logical_not(outer))
-    def _():
-        relay(before - 1)
-
-        if helps:
-            for b in early:
-                side(b)
-
-        @pl.loop(before, CHUNKS)
-        def _(i):
-            @pl.when(f == 1)
-            def _():
-                pass_up(1, i)
-
-            @pl.when(f == n_fib - 2)
-            def _():
-                pass_down(1, i)
-
-        if helps:
-            for b in range(len(early), parts):
-                side(b)
+        near(half)
 
     gather(parts - 1)
 
@@ -343,21 +334,21 @@
         def _():
             came_pair(other, parts).wait_recv()
 
-    def product(ref, part, col, k):
+    def products(ref, part, first, count):
         return jnp.dot(
-            left[k, part, :],
-            ref[
-                pl.ds(pl.multiple_of(k * unit, unit), unit),
-                pl.ds(pl.multiple_of(col * unit, unit), unit),
-            ],
+            jnp.concatenate([left[first + k, part, :] for k in range(count)], axis=1),
+            ref[pl.ds(first * unit if isinstance(first, int) else pl.multiple_of(first * unit, unit), count * unit), :],
             preferred_element_type=jnp.float32,
         )
 
-    def all_products(part, col):
-        total = product(right, part, col, 0)
-        for k in range(1, n_fib):
-            total += product(right, part, col, k)
-        return total
+    def store(total, ours, part, out):
+        kept_total = total[:, :unit]
+        for col in range(n_col):
+            piece = total[:, col * unit:(col + 1) * unit]
+            out[col, part, :] = piece.astype(jnp.bfloat16)
+            if col:
+                kept_total = jnp.where(c == col, piece, kept_total)
+        ours[part, :] = kept_total
 
     def col_at(shift):
         return lax.rem(c + shift, n_col)
@@ -398,36 +389,41 @@
                 def _():
                     came_far_pair(other, parts - skipped).wait_recv()
 
-        reckon(0, lead)
-
-    def reckon(h, count):
-        if count == 0:
-            return
-        part = pl.ds(lent_at(h) * step, count * step)
-        there = pl.ds(h * step, count * step)
-        for shift in list(range(1, n_col)) + [0]:
-            col = col_at(shift)
-            total = product(right_far, part, col, lax.rem(mate + 1, n_fib))
-            for k in range(2, n_fib):
-                total += product(right_far, part, col, lax.rem(mate + k, n_fib))
-            if shift:
-                help_out[col, there, :] = total.astype(jnp.bfloat16)
-                for i in range(h, h + count):
-                    to_help(col, i).start()
-            else:
-                help_own[there, :] = total
+        part = pl.ds(0, helps * step)
+        total = products(right_far, part, jnp.where(mate == 0, 1, 0), n_fib - 1)
+        store(total, help_own, part, help_out)
+        for i in range(helps):
+            for shift in range(1, n_col):
+                to_help(col_at(shift), i).start()
 
     if helps:
         @pl.when(outer)
         def _():
             for h in range(helps):
-                i = lent_at(h)
+                i = h
                 part = pl.ds(i * step, step)
+                store(products(right, part, f, 1), own, part, part_out)
                 for shift in range(1, n_col):
-                    col = col_at(shift)
-                    part_out[col, part, :] = product(right, part, col, f).astype(jnp.bfloat16)
-                    to_col(col, i).start()
-                own[part, :] = product(right, part, c, f)
+                    to_col(col_at(shift), i).start()
+
+    def advance(i):
+        odd = lax.rem(i, 2) == 1
+
+        @pl.when((i < CHUNKS - 5) & jnp.logical_not(odd))
+        def _():
+            far(half - 2 + i // 2)
+
+        @pl.when((i < CHUNKS - 5) & odd)
+        def _():
+            near(half + 1 + i // 2)
+
+        @pl.when((i == CHUNKS - 5) | (i == CHUNKS - 4))
+        def _():
+            near(i + 3)
+
+        @pl.when((i >= CHUNKS - 5) & (i < CHUNKS - 1))
+        def _():
+            far(i + 1)
 
     @pl.loop(0, CHUNKS)
     def _(i):
@@ -441,31 +437,28 @@
                 pass_down(d, i)
 
         if helps:
+            @pl.when(helper & (i == ANSWER))
+            def _():
+                answer()
+
+        @pl.when(inner & (i == ANSWER))
+        def _():
+            advance(i)
+
+        @pl.when(full)
+        def _():
+            store(products(right, part, 0, n_fib), own, part, part_out)
+            for shift in range(1, n_col):
+                to_col(col_at(shift), i).start()
+
+        if helps:
             @pl.when(helper & (i == FETCH))
             def _():
                 fetch()
 
-            @pl.when(helper & (i == ANSWER))
-            def _():
-                answer()
-
-            for h in range(lead, helps):
-                @pl.when(helper & (i == lent_at(h)))
-                def _():
-                    reckon(h, 1)
-
-        @pl.when(full)
-        def _():
-            for shift in range(1, n_col):
-                col = col_at(shift)
-                part_out[col, part, :] = all_products(part, col).astype(jnp.bfloat16)
-                to_col(col, i).start()
-
-            own[part, :] = all_products(part, c)
-
-        @pl.when(jnp.logical_not(outer) & (i + before < CHUNKS + last))
-        def _():
-            relay(i + before)
+        @pl.when(inner & (i != ANSWER))
+        def _():
+            advance(i)
 
         @pl.when((i >= LAG) & (kept(i - LAG) | jnp.logical_not(outer)))
         def _():
@@ -482,23 +475,18 @@
             helped[part, :] = total.astype(jnp.bfloat16)
             to_done(h).start()
 
-    for h in range(lead):
+    for h in range(helps):
         reply(h)
 
-    for i in range(CHUNKS - LAG, CHUNKS):
-        for h in range(lead, helps):
-            if lent_at(h) == i:
-                reply(h)
-
-        @pl.when(kept(jnp.asarray(i)) | jnp.logical_not(outer))
-        def _():
-            combine(i)
+    @pl.loop(CHUNKS - LAG, CHUNKS)
+    def _(i):
+        combine(i)
 
     if helps:
         @pl.when(outer)
         def _():
             for h in range(helps):
-                combine(lent_at(h), h)
+                combine(h, h)
 
     def to_row(shift):
         return pltpu.make_async_remote_copy(

time: 48.8 us -> 46.9 us (0.961)
  Pallas kernels: 48.6 us -> 46.7 us
    pallas_call x1, Pallas kernels: 47 us -> 45.1 us  [local(): pl.pallas_call(functools.partial(kernel, n_row, n_col, n_fib, helps), out...]
where the time goes in v4:
time: 46.9 us; the launch traced here: 46.8 us
  Pallas kernels  46.7 us (100%)
    pallas_call x1, Pallas kernels, local(): pl.pallas_call(functools.partial(kernel, n_row, n_col, n_fib, helps), out...  45.1 us
    pallas_call x1, Pallas kernels, local(): pl.pallas_call(prune, out_shape=jax.ShapeDtypeStruct((rows, unit), jnp.fl...  1.64 us

profile of v4, /device:TPU:0, one launch (start us, length us, event | category | flops | bytes accessed | tf_op | source)
XLA Modules:
  0.0 46.8 jit_solution(2080599385620121480)
XLA Ops:
  0.0 0.0 copy-start
  0.0 45.1 %expand.1 = (f32[768,384]{1,0:T(8,128)S(1)}, f32[8,384]{1,0:T(8,128)S(1)}) custom-call(s32[3,6]{1,0:T(4,128)} %bitcast.3, f32[768,384]{1,0:T(8,128)} %values_hbm.1), custom_call_target="tpu_custom_call" | custom-call | tf_op jit(solution)/shard_map/expand/pallas_call | solution.py:593
  45.1 0.0 copy-done
  45.1 1.6 %prune.1 = f32[768,384]{1,0:T(8,128)} custom-call(s32[3,6]{1,0:T(4,128)S(1)} %bitcast.2, f32[768,384]{1,0:T(8,128)S(1)} %get-tuple-element.7.squared_ref, f32[8,384]{1,0:T(8,128)S(1)} %get-tuple-element.8.inverse_ref), custom_call_target="tpu_custom_call" | custom-call | tf_op jit(solution)/shard_map/prune/pallas_call | solution.py:645
Async XLA Ops:
  0.0 45.1 %copy-start = (s32[6,3]{0,1:T(4,128)S(1)}, s32[6,3]{0,1:T(4,128)}, u32[]{:S(2)}) copy-start(s32[6,3]{0,1:T(4,128)} %param.5) | copy-start | bytes 220

commit v5 on v4

--- a/solution.py
+++ b/solution.py
@@ -10,6 +10,7 @@
 MESH = pl.DeviceIdType.MESH
 CHUNKS = 12
 HELP = 3
+TRAIL = 1
 AHEAD = 3
 FETCH = 8
 ANSWER = 9
@@ -21,7 +22,7 @@
     n_row, n_col, n_fib, helps, tile_hbm, values_hbm, own, inverse_ref,
     tile_ref, values_ref, left, right, part_out, part_in, sums,
     right_far, help_own, help_out, help_in, helped, load_sem,
-    sent_left, sent_right, sent_pair, sent_part, sent_sum, sent_far, sent_far_pair, sent_help, sent_done,
+    sent_left, sent_right, sent_pair, sent_part, sent_sum, sent_far, sent_far_pair, sent_help, sent_done, sent_owner,
     recv_left, recv_right, recv_pair, recv_part, recv_sum,
     recv_far, recv_far_pair, recv_help, recv_done,
 ):
@@ -84,8 +85,14 @@
             device_id=(r, c, f + 1 if up else f - 1), device_id_type=MESH,
         )
 
+    late = min(helps, TRAIL)
+    lead = helps - late
+
     def kept(i):
-        return i >= helps
+        return (i >= lead) & (i < CHUNKS - late)
+
+    def lent_at(h):
+        return h if h < lead else h - helps + CHUNKS
 
     def sends_up(i):
         return has_up & (kept(i) | (f + 1 < n_fib - 1))
@@ -192,6 +199,20 @@
 
     def skips(place, far):
         return (far >= place * parts) & (far < (place + 1) * parts)
+
+    def to_owner(col, i):
+        return pltpu.make_async_remote_copy(
+            src_ref=help_out.at[col, chunk(i)], dst_ref=help_in.at[c, chunk(i)],
+            send_sem=sent_owner.at[0], recv_sem=recv_done.at[i],
+            device_id=(r, col, mate), device_id_type=MESH,
+        )
+
+    def came_owner(i):
+        all_cols = help_in.at[pl.ds(0, n_col), chunk(i)]
+        return pltpu.make_async_remote_copy(
+            src_ref=all_cols, dst_ref=all_cols, send_sem=sent_owner.at[0], recv_sem=recv_done.at[i],
+            device_id=(r, c, f), device_id_type=MESH,
+        )
 
     def served(place, b):
         return place * parts + b != mate
@@ -361,7 +382,11 @@
         for shift in range(1, n_col):
             came_col(col_at(shift), i).wait_recv()
             expanded += part_in[col_at(shift), part, :].astype(jnp.float32)
-        if h is not None:
+        if h is not None and h >= lead:
+            came_owner(h).wait_recv()
+            for col in range(n_col):
+                expanded += help_in[col, pl.ds(h * step, step), :].astype(jnp.float32)
+        elif h is not None:
             to_done(h).wait_recv()
             expanded += helped[pl.ds(h * step, step), :].astype(jnp.float32)
         squared = expanded * expanded
@@ -389,18 +414,24 @@
                 def _():
                     came_far_pair(other, parts - skipped).wait_recv()
 
-        part = pl.ds(0, helps * step)
+        reckon(0, lead)
+
+    def reckon(h, count):
+        part = pl.ds(lent_at(h) * step, count * step)
         total = products(right_far, part, jnp.where(mate == 0, 1, 0), n_fib - 1)
-        store(total, help_own, part, help_out)
-        for i in range(helps):
-            for shift in range(1, n_col):
-                to_help(col_at(shift), i).start()
+        store(total, help_own, pl.ds(h * step, count * step), help_out)
+        for i in range(h, h + count):
+            for shift in range(n_col):
+                if h >= lead:
+                    to_owner(col_at(shift), i).start()
+                elif shift:
+                    to_help(col_at(shift), i).start()
 
     if helps:
         @pl.when(outer)
         def _():
             for h in range(helps):
-                i = h
+                i = lent_at(h)
                 part = pl.ds(i * step, step)
                 store(products(right, part, f, 1), own, part, part_out)
                 for shift in range(1, n_col):
@@ -441,9 +472,14 @@
             def _():
                 answer()
 
-        @pl.when(inner & (i == ANSWER))
+        @pl.when(inner & ((i == ANSWER) | (i == CHUNKS - 2)))
         def _():
             advance(i)
+
+        if late:
+            @pl.when(helper & (i == CHUNKS - 2))
+            def _():
+                reckon(lead, late)
 
         @pl.when(full)
         def _():
@@ -456,7 +492,7 @@
             def _():
                 fetch()
 
-        @pl.when(inner & (i != ANSWER))
+        @pl.when(inner & (i != ANSWER) & (i != CHUNKS - 2))
         def _():
             advance(i)
 
@@ -475,18 +511,20 @@
             helped[part, :] = total.astype(jnp.bfloat16)
             to_done(h).start()
 
-    for h in range(helps):
+    for h in range(lead):
         reply(h)
 
     @pl.loop(CHUNKS - LAG, CHUNKS)
     def _(i):
-        combine(i)
+        @pl.when(kept(i) | inner)
+        def _():
+            combine(i)
 
     if helps:
         @pl.when(outer)
         def _():
             for h in range(helps):
-                combine(h, h)
+                combine(lent_at(h), h)
 
     def to_row(shift):
         return pltpu.make_async_remote_copy(
@@ -559,9 +597,12 @@
 
         @pl.when(helper)
         def _():
-            if n_col > 1:
-                left_behind(sent_help.at[0], help_out.at[pl.ds(0, n_col - 1)])
-            left_behind(sent_done.at[0], helped)
+            if lead:
+                if n_col > 1:
+                    left_behind(sent_help.at[0], help_out.at[pl.ds(0, n_col - 1), pl.ds(0, lead * step)])
+                left_behind(sent_done.at[0], helped.at[pl.ds(0, lead * step)])
+            if late:
+                left_behind(sent_owner.at[0], help_out.at[pl.ds(0, n_col), pl.ds(lead * step, late * step)])
 
 
 def prune(keep_ref, squared_ref, inverse_ref, out_hbm, out_vmem, sem):
@@ -627,6 +668,7 @@
                 dma((1,)),
                 dma((1,)),
                 dma((1,)),
+                dma((1,)),
                 dma((n_fib - 1, CHUNKS)),
                 dma((n_col, parts)),
                 dma((group,)),

time: 46.9 us -> 45.7 us (0.974)
  Pallas kernels: 46.7 us -> 45.5 us
    pallas_call x1, Pallas kernels: 45.1 us -> 43.9 us  [local(): pl.pallas_call(functools.partial(kernel, n_row, n_col, n_fib, helps), out...]
where the time goes in v5:
time: 45.7 us; the launch traced here: 45.6 us
  Pallas kernels  45.5 us (100%)
    pallas_call x1, Pallas kernels, local(): pl.pallas_call(functools.partial(kernel, n_row, n_col, n_fib, helps), out...  43.9 us
    pallas_call x1, Pallas kernels, local(): pl.pallas_call(prune, out_shape=jax.ShapeDtypeStruct((rows, unit), jnp.fl...  1.64 us

profile of v5, /device:TPU:0, one launch (start us, length us, event | category | flops | bytes accessed | tf_op | source)
XLA Modules:
  0.0 45.6 jit_solution(7350834780901810396)
XLA Ops:
  0.0 0.0 copy-start
  0.0 43.9 %expand.1 = (f32[768,384]{1,0:T(8,128)S(1)}, f32[8,384]{1,0:T(8,128)S(1)}) custom-call(s32[3,6]{1,0:T(4,128)} %bitcast.3, f32[768,384]{1,0:T(8,128)} %values_hbm.1), custom_call_target="tpu_custom_call" | custom-call | tf_op jit(solution)/shard_map/expand/pallas_call | solution.py:634
  43.9 0.0 copy-done
  43.9 1.6 %prune.1 = f32[768,384]{1,0:T(8,128)} custom-call(s32[3,6]{1,0:T(4,128)S(1)} %bitcast.2, f32[768,384]{1,0:T(8,128)S(1)} %get-tuple-element.7.squared_ref, f32[8,384]{1,0:T(8,128)S(1)} %get-tuple-element.8.inverse_ref), custom_call_target="tpu_custom_call" | custom-call | tf_op jit(solution)/shard_map/prune/pallas_call | solution.py:687
Async XLA Ops:
  0.0 43.9 %copy-start = (s32[6,3]{0,1:T(4,128)S(1)}, s32[6,3]{0,1:T(4,128)}, u32[]{:S(2)}) copy-start(s32[6,3]{0,1:T(4,128)} %param.5) | copy-start | bytes 220

commit v6 on v5

--- a/solution.py
+++ b/solution.py
@@ -11,8 +11,8 @@
 CHUNKS = 12
 HELP = 3
 TRAIL = 1
-AHEAD = 3
-FETCH = 8
+AHEAD = 4
+FETCH = 7
 ANSWER = 9
 LAG = 4
 VMEM_LIMIT = 62 * 1024 * 1024
@@ -20,7 +20,7 @@
 
 def kernel(
     n_row, n_col, n_fib, helps, tile_hbm, values_hbm, own, inverse_ref,
-    tile_ref, values_ref, left, right, part_out, part_in, sums,
+    tile_ref, values_ref, left, right, part_out, part_in, folded, sums,
     right_far, help_own, help_out, help_in, helped, load_sem,
     sent_left, sent_right, sent_pair, sent_part, sent_sum, sent_far, sent_far_pair, sent_help, sent_done, sent_owner,
     recv_left, recv_right, recv_pair, recv_part, recv_sum,
@@ -374,7 +374,7 @@
     def col_at(shift):
         return lax.rem(c + shift, n_col)
 
-    sums[r] = jnp.zeros((8, unit), jnp.float32)
+    folded[...] = jnp.zeros((8, unit), jnp.float32)
 
     def combine(i, h=None):
         part = chunk(i)
@@ -391,7 +391,7 @@
             expanded += helped[pl.ds(h * step, step), :].astype(jnp.float32)
         squared = expanded * expanded
         own[part, :] = squared
-        sums[r] += jnp.sum(squared.reshape(step // 8, 8, unit), axis=0)
+        folded[...] += jnp.sum(squared.reshape(step // 8, 8, unit), axis=0)
 
     def fetch():
         for b in range(parts):
@@ -440,17 +440,17 @@
     def advance(i):
         odd = lax.rem(i, 2) == 1
 
+        @pl.when(i == 0)
+        def _():
+            near(half + 1)
+
         @pl.when((i < CHUNKS - 5) & jnp.logical_not(odd))
         def _():
             far(half - 2 + i // 2)
 
-        @pl.when((i < CHUNKS - 5) & odd)
-        def _():
-            near(half + 1 + i // 2)
-
-        @pl.when((i == CHUNKS - 5) | (i == CHUNKS - 4))
-        def _():
-            near(i + 3)
+        @pl.when((i <= CHUNKS - 5) & odd)
+        def _():
+            near(half + 2 + i // 2)
 
         @pl.when((i >= CHUNKS - 5) & (i < CHUNKS - 1))
         def _():
@@ -540,13 +540,14 @@
             device_id=(r, c, f), device_id_type=MESH,
         )
 
+    sums[r] = jnp.sum(folded[...], axis=0, keepdims=True)
     for shift in range(1, n_row):
         to_row(shift).start()
     came_rows().wait_recv()
     total = sums[0]
     for other in range(1, n_row):
         total += sums[other]
-    scale = jnp.sum(total, axis=0, keepdims=True) / (rows * n_row) + 1e-6
+    scale = total / (rows * n_row) + 1e-6
     inverse_ref[...] = jnp.broadcast_to(1.0 / scale, inverse_ref.shape)
 
     def left_behind(sem, ref):
@@ -652,7 +653,8 @@
                 pltpu.VMEM((group * rows, n_col * unit), jnp.bfloat16),
                 pltpu.VMEM((n_col, rows, unit), jnp.bfloat16),
                 pltpu.VMEM((n_col, rows, unit), jnp.bfloat16),
-                pltpu.VMEM((n_row, 8, unit), jnp.float32),
+                pltpu.VMEM((8, unit), jnp.float32),
+                pltpu.VMEM((n_row, 1, unit), jnp.float32),
                 pltpu.VMEM((group * rows, n_col * unit), jnp.bfloat16),
                 pltpu.VMEM((few, unit), jnp.float32),
                 pltpu.VMEM((n_col, few, unit), jnp.bfloat16),

time: 45.7 us -> 44.7 us (0.978)
  Pallas kernels: 45.5 us -> 44.5 us
    pallas_call x1, Pallas kernels: 43.9 us -> 42.9 us  [local(): pl.pallas_call(functools.partial(kernel, n_row, n_col, n_fib, helps), out...]
where the time goes in v6:
time: 44.7 us; the launch traced here: 44.5 us
  Pallas kernels  44.5 us (100%)
    pallas_call x1, Pallas kernels, local(): pl.pallas_call(functools.partial(kernel, n_row, n_col, n_fib, helps), out...  42.9 us
    pallas_call x1, Pallas kernels, local(): pl.pallas_call(prune, out_shape=jax.ShapeDtypeStruct((rows, unit), jnp.fl...  1.64 us

profile of v6, /device:TPU:0, one launch (start us, length us, event | category | flops | bytes accessed | tf_op | source)
XLA Modules:
  0.0 44.5 jit_solution(1834612187578119344)
XLA Ops:
  0.0 0.0 copy-start
  0.0 42.9 %expand.1 = (f32[768,384]{1,0:T(8,128)S(1)}, f32[8,384]{1,0:T(8,128)S(1)}) custom-call(s32[3,6]{1,0:T(4,128)} %bitcast.3, f32[768,384]{1,0:T(8,128)} %values_hbm.1), custom_call_target="tpu_custom_call" | custom-call | tf_op jit(solution)/shard_map/expand/pallas_call | solution.py:635
  42.9 0.0 copy-done
  42.9 1.6 %prune.1 = f32[768,384]{1,0:T(8,128)} custom-call(s32[3,6]{1,0:T(4,128)S(1)} %bitcast.2, f32[768,384]{1,0:T(8,128)S(1)} %get-tuple-element.7.squared_ref, f32[8,384]{1,0:T(8,128)S(1)} %get-tuple-element.8.inverse_ref), custom_call_target="tpu_custom_call" | custom-call | tf_op jit(solution)/shard_map/prune/pallas_call | solution.py:689
Async XLA Ops:
  0.0 42.9 %copy-start = (s32[6,3]{0,1:T(4,128)S(1)}, s32[6,3]{0,1:T(4,128)}, u32[]{:S(2)}) copy-start(s32[6,3]{0,1:T(4,128)} %param.5) | copy-start | bytes 220

commit v7 on v6

--- a/solution.py
+++ b/solution.py
@@ -19,8 +19,8 @@
 
 
 def kernel(
-    n_row, n_col, n_fib, helps, tile_hbm, values_hbm, own, inverse_ref,
-    tile_ref, values_ref, left, right, part_out, part_in, folded, sums,
+    n_row, n_col, n_fib, helps, tile_hbm, keep_hbm, values_hbm, own, factor_ref,
+    tile_ref, keep_ref, values_ref, left, right, part_out, part_in, folded, sums,
     right_far, help_own, help_out, help_in, helped, load_sem,
     sent_left, sent_right, sent_pair, sent_part, sent_sum, sent_far, sent_far_pair, sent_help, sent_done, sent_owner,
     recv_left, recv_right, recv_pair, recv_part, recv_sum,
@@ -38,6 +38,8 @@
     load.start()
     load_tile = pltpu.make_async_copy(tile_hbm, tile_ref, load_sem.at[1])
     load_tile.start()
+    load_keep = pltpu.make_async_copy(keep_hbm, keep_ref, load_sem.at[2])
+    load_keep.start()
 
     barrier = pltpu.get_barrier_semaphore()
     for dr in range(n_row):
@@ -63,6 +65,7 @@
         pl.semaphore_signal(barrier, inc=1, device_id=(r, c, f + 1), device_id_type=MESH)
 
     load_tile.wait()
+    load_keep.wait()
     load.wait()
 
     for i in range(rows // tile):
@@ -414,7 +417,8 @@
                 def _():
                     came_far_pair(other, parts - skipped).wait_recv()
 
-        reckon(0, lead)
+        if lead:
+            reckon(0, lead)
 
     def reckon(h, count):
         part = pl.ds(lent_at(h) * step, count * step)
@@ -472,14 +476,14 @@
             def _():
                 answer()
 
-        @pl.when(inner & ((i == ANSWER) | (i == CHUNKS - 2)))
+        @pl.when(inner & (i >= ANSWER))
         def _():
             advance(i)
 
-        if late:
-            @pl.when(helper & (i == CHUNKS - 2))
-            def _():
-                reckon(lead, late)
+        for h in range(lead, helps):
+            @pl.when(helper & (i == max(lent_at(h) - 1, ANSWER)))
+            def _():
+                reckon(h, 1)
 
         @pl.when(full)
         def _():
@@ -492,7 +496,7 @@
             def _():
                 fetch()
 
-        @pl.when(inner & (i != ANSWER) & (i != CHUNKS - 2))
+        @pl.when(inner & (i < ANSWER))
         def _():
             advance(i)
 
@@ -548,7 +552,11 @@
     for other in range(1, n_row):
         total += sums[other]
     scale = total / (rows * n_row) + 1e-6
-    inverse_ref[...] = jnp.broadcast_to(1.0 / scale, inverse_ref.shape)
+    inverse = 1.0 / scale
+    for i in range(rows // tile):
+        for j in range(unit // tile):
+            across = slice(j * tile, (j + 1) * tile)
+            factor_ref[i:i + 1, across] = inverse[:, across] * keep_ref[j, i].astype(jnp.float32)
 
     def left_behind(sem, ref):
         pltpu.make_async_remote_copy(
@@ -606,15 +614,12 @@
                 left_behind(sent_owner.at[0], help_out.at[pl.ds(0, n_col), pl.ds(lead * step, late * step)])
 
 
-def prune(keep_ref, squared_ref, inverse_ref, out_hbm, out_vmem, sem):
-    tile = out_vmem.shape[1] // keep_ref.shape[0]
+def prune(squared_ref, factor_ref, out_hbm, out_vmem, sem):
+    tile = out_vmem.shape[0] // factor_ref.shape[0]
     copies = []
-    for i in range(keep_ref.shape[1]):
+    for i in range(factor_ref.shape[0]):
         down = slice(i * tile, (i + 1) * tile)
-        for j in range(keep_ref.shape[0]):
-            across = slice(j * tile, (j + 1) * tile)
-            factor = inverse_ref[0:1, across] * keep_ref[j, i].astype(jnp.float32)
-            out_vmem[down, across] = squared_ref[down, across] * factor
+        out_vmem[down] = squared_ref[down] * factor_ref[i:i + 1]
         copy = pltpu.make_async_copy(out_vmem.at[down], out_hbm.at[down], sem.at[i])
         copy.start()
         copies.append(copy)
@@ -632,13 +637,14 @@
         dma = pltpu.SemaphoreType.DMA
         parts = rows // unit
         few = rows // CHUNKS * HELP
-        squared, inverse = pl.pallas_call(
+        squared, factor = pl.pallas_call(
             functools.partial(kernel, n_row, n_col, n_fib, helps),
             out_shape=(
                 pltpu.VMEM((rows, unit), jnp.float32),
-                pltpu.VMEM((8, unit), jnp.float32),
+                pltpu.VMEM((tile_mask.shape[0], unit), jnp.float32),
             ),
             in_specs=[
+                pl.BlockSpec(memory_space=pltpu.HBM),
                 pl.BlockSpec(memory_space=pltpu.HBM),
                 pl.BlockSpec(memory_space=pltpu.HBM),
             ],
@@ -648,6 +654,7 @@
             ),
             scratch_shapes=[
                 pltpu.SMEM(tile_mask.shape[::-1], jnp.int32),
+                pltpu.SMEM(keep_mask.shape[::-1], jnp.int32),
                 pltpu.VMEM((rows, unit), jnp.float32),
                 pltpu.VMEM((n_fib, rows, unit), jnp.bfloat16),
                 pltpu.VMEM((group * rows, n_col * unit), jnp.bfloat16),
@@ -660,7 +667,7 @@
                 pltpu.VMEM((n_col, few, unit), jnp.bfloat16),
                 pltpu.VMEM((n_col, few, unit), jnp.bfloat16),
                 pltpu.VMEM((few, unit), jnp.bfloat16),
-                dma((2,)),
+                dma((3,)),
                 dma((2,)),
                 dma((1,)),
                 dma((1,)),
@@ -685,12 +692,11 @@
                 collective_id=0, has_side_effects=True, vmem_limit_bytes=VMEM_LIMIT
             ),
             name="expand",
-        )(tile_mask.T, values)
+        )(tile_mask.T, keep_mask.T, values)
         return pl.pallas_call(
             prune,
             out_shape=jax.ShapeDtypeStruct((rows, unit), jnp.float32),
             in_specs=[
-                pl.BlockSpec(memory_space=pltpu.SMEM),
                 pl.BlockSpec(memory_space=pltpu.VMEM),
                 pl.BlockSpec(memory_space=pltpu.VMEM),
             ],
@@ -701,7 +707,7 @@
             ],
             compiler_params=pltpu.CompilerParams(vmem_limit_bytes=8 * 1024 * 1024),
             name="prune",
-        )(keep_mask.T, squared, inverse)
+        )(squared, factor)
 
     spec = P("row", ("col", "fiber"))
     return jax.shard_map(

time: 44.7 us -> 44.1 us (0.987)
  Pallas kernels: 44.5 us -> 44 us
    pallas_call x1, Pallas kernels: 1.64 us -> 1.07 us  [local(): pl.pallas_call(prune, out_shape=jax.ShapeDtypeStruct((rows, unit), jnp.fl...]
where the time goes in v7:
time: 44.1 us; the launch traced here: 44 us
  Pallas kernels  44 us (100%)
    pallas_call x1, Pallas kernels, local(): pl.pallas_call(functools.partial(kernel, n_row, n_col, n_fib, helps), out...  42.9 us
    pallas_call x1, Pallas kernels, local(): pl.pallas_call(prune, out_shape=jax.ShapeDtypeStruct((rows, unit), jnp.fl...  1.07 us

profile of v7, /device:TPU:0, one launch (start us, length us, event | category | flops | bytes accessed | tf_op | source)
XLA Modules:
  0.0 44.0 jit_solution(4505069183643245240)
XLA Ops:
  0.0 42.9 %expand.1 = (f32[768,384]{1,0:T(8,128)S(1)}, f32[6,384]{1,0:T(8,128)S(1)}) custom-call(s32[3,6]{1,0:T(4,128)} %bitcast.2, s32[3,6]{1,0:T(4,128)} %bitcast.3, f32[768,384]{1,0:T(8,128)} %values_hbm.1), custom_call_target="tpu_custom_call" | custom-call | tf_op jit(solution)/shard_map/expand/pallas_call | solution.py:640
  42.9 1.1 %prune.1 = f32[768,384]{1,0:T(8,128)} custom-call(f32[768,384]{1,0:T(8,128)S(1)} %get-tuple-element.7.squared_ref, f32[6,384]{1,0:T(8,128)S(1)} %get-tuple-element.8.factor_ref), custom_call_target="tpu_custom_call" | custom-call | tf_op jit(solution)/shard_map/prune/pallas_call | solution.py:696

commit v8 on v7

--- a/solution.py
+++ b/solution.py
@@ -12,17 +12,18 @@
 HELP = 3
 TRAIL = 1
 AHEAD = 4
+FIRST_FETCH = 4
 FETCH = 7
 ANSWER = 9
-LAG = 4
+LAG = 5
 VMEM_LIMIT = 62 * 1024 * 1024
 
 
 def kernel(
     n_row, n_col, n_fib, helps, tile_hbm, keep_hbm, values_hbm, own, factor_ref,
-    tile_ref, keep_ref, values_ref, left, right, part_out, part_in, folded, sums,
+    tile_ref, keep_ref, values_ref, left, right, part_out, part_in, folded, sums, partial,
     right_far, help_own, help_out, help_in, helped, load_sem,
-    sent_left, sent_right, sent_pair, sent_part, sent_sum, sent_far, sent_far_pair, sent_help, sent_done, sent_owner,
+    sent_left, sent_right, sent_pair, sent_part, sent_sum, sent_far, sent_helper,
     recv_left, recv_right, recv_pair, recv_part, recv_sum,
     recv_far, recv_far_pair, recv_help, recv_done,
 ):
@@ -121,36 +122,33 @@
     def to_right(t, b):
         return pltpu.make_async_remote_copy(
             src_ref=block(f, b), dst_ref=right_at(right, c, seat, b),
-            send_sem=sent_right.at[0], recv_sem=recv_right.at[c, b],
+            send_sem=sent_right.at[0], recv_sem=recv_right.at[b],
             device_id=(t * group + seat, owner, f), device_id_type=MESH,
         )
 
-    def came_right(col, b):
-        return pltpu.make_async_remote_copy(
-            src_ref=block(f, b), dst_ref=right_at(right, col, seat, b),
-            send_sem=sent_right.at[0], recv_sem=recv_right.at[col, b],
-            device_id=(r, c, f), device_id_type=MESH,
-        )
+    def arrived(ref, recv, b):
+        for less in range(2):
+            if n_col > less:
+                @pl.when(mine == bool(less))
+                def _():
+                    theirs = ref.at[pl.ds(0, unit), pl.ds(0, (n_col - less) * unit)]
+                    pltpu.make_async_remote_copy(
+                        src_ref=theirs, dst_ref=theirs, send_sem=sent_right.at[0],
+                        recv_sem=recv.at[b], device_id=(r, c, f), device_id_type=MESH,
+                    ).wait_recv()
 
     def to_far(col, b):
         return pltpu.make_async_remote_copy(
             src_ref=right_at(right, col, seat, b), dst_ref=right_at(right_far, col, seat, b),
-            send_sem=sent_far.at[0], recv_sem=recv_far.at[col, b],
+            send_sem=sent_far.at[0], recv_sem=recv_far.at[b],
             device_id=(r, c, mate), device_id_type=MESH,
         )
 
     def to_side(t, b):
         return pltpu.make_async_remote_copy(
             src_ref=block(mate, b), dst_ref=right_at(right_far, c, seat, b),
-            send_sem=sent_far.at[0], recv_sem=recv_far.at[c, b],
+            send_sem=sent_far.at[0], recv_sem=recv_far.at[b],
             device_id=(t * group + seat, c, f), device_id_type=MESH,
-        )
-
-    def came_far(col, b):
-        return pltpu.make_async_remote_copy(
-            src_ref=block(f, b), dst_ref=right_at(right_far, col, seat, b),
-            send_sem=sent_far.at[0], recv_sem=recv_far.at[col, b],
-            device_id=(r, c, f), device_id_type=MESH,
         )
 
     def pairing(ref, send, recv):
@@ -171,32 +169,34 @@
         return to_pair, came_pair
 
     to_pair, came_pair = pairing(right, sent_pair, recv_pair)
-    to_far_pair, came_far_pair = pairing(right_far, sent_far_pair, recv_far_pair)
-
-    def crossing(out, into, send, recv):
+    to_far_pair, came_far_pair = pairing(right_far, sent_helper, recv_far_pair)
+
+    def crossing(out, into, send, recv, share):
         def to_col(col, i):
             return pltpu.make_async_remote_copy(
                 src_ref=out.at[col, chunk(i)], dst_ref=into.at[c, chunk(i)],
-                send_sem=send.at[0], recv_sem=recv.at[lax.rem(c - col + n_col, n_col) - 1, i],
+                send_sem=send.at[0],
+                recv_sem=recv.at[lax.rem(c - col + n_col, n_col) - 1, i // share],
                 device_id=(r, col, f), device_id_type=MESH,
             )
 
         def came_col(col, i):
+            both = into.at[col, pl.ds(i * step, share * step)]
             return pltpu.make_async_remote_copy(
-                src_ref=out.at[col, chunk(i)], dst_ref=into.at[col, chunk(i)],
-                send_sem=send.at[0], recv_sem=recv.at[lax.rem(col - c + n_col, n_col) - 1, i],
+                src_ref=both, dst_ref=both, send_sem=send.at[0],
+                recv_sem=recv.at[lax.rem(col - c + n_col, n_col) - 1, i // share],
                 device_id=(r, col, f), device_id_type=MESH,
             )
 
         return to_col, came_col
 
-    to_col, came_col = crossing(part_out, part_in, sent_part, recv_part)
-    to_help, came_help = crossing(help_out, help_in, sent_help, recv_help)
+    to_col, came_col = crossing(part_out, part_in, sent_part, recv_part, 2)
+    to_help, came_help = crossing(help_out, help_in, sent_helper, recv_help, 1)
 
     def to_done(i):
         return pltpu.make_async_remote_copy(
             src_ref=helped.at[chunk(i)], dst_ref=helped.at[chunk(i)],
-            send_sem=sent_done.at[0], recv_sem=recv_done.at[i],
+            send_sem=sent_helper.at[0], recv_sem=recv_done.at[i],
             device_id=(r, c, mate), device_id_type=MESH,
         )
 
@@ -206,14 +206,14 @@
     def to_owner(col, i):
         return pltpu.make_async_remote_copy(
             src_ref=help_out.at[col, chunk(i)], dst_ref=help_in.at[c, chunk(i)],
-            send_sem=sent_owner.at[0], recv_sem=recv_done.at[i],
+            send_sem=sent_helper.at[0], recv_sem=recv_done.at[i],
             device_id=(r, col, mate), device_id_type=MESH,
         )
 
     def came_owner(i):
         all_cols = help_in.at[pl.ds(0, n_col), chunk(i)]
         return pltpu.make_async_remote_copy(
-            src_ref=all_cols, dst_ref=all_cols, send_sem=sent_owner.at[0], recv_sem=recv_done.at[i],
+            src_ref=all_cols, dst_ref=all_cols, send_sem=sent_helper.at[0], recv_sem=recv_done.at[i],
             device_id=(r, c, f), device_id_type=MESH,
         )
 
@@ -310,11 +310,8 @@
             spot[...] = left[mate, b * unit:(b + 1) * unit]
 
     def gather(b):
+        arrived(right, recv_right, b)
         for col in range(n_col):
-            @pl.when(jnp.logical_not(mine & (c == col)))
-            def _():
-                came_right(col, b).wait_recv()
-
             if helps:
                 @pl.when(outer & (c != col) & to_serve(b))
                 def _():
@@ -382,8 +379,16 @@
     def combine(i, h=None):
         part = chunk(i)
         expanded = own[part, :]
+        def await_two():
+            for shift in range(1, n_col):
+                came_col(col_at(shift), i).wait_recv()
+
+        if not isinstance(i, int):
+            pl.when(lax.rem(i, 2) == 0)(await_two)
+        elif i % 2 == 0:
+            await_two()
+
         for shift in range(1, n_col):
-            came_col(col_at(shift), i).wait_recv()
             expanded += part_in[col_at(shift), part, :].astype(jnp.float32)
         if h is not None and h >= lead:
             came_owner(h).wait_recv()
@@ -396,19 +401,15 @@
         own[part, :] = squared
         folded[...] += jnp.sum(squared.reshape(step // 8, 8, unit), axis=0)
 
-    def fetch():
-        for b in range(parts):
-            @pl.when(served(seat, b))
-            def _():
-                for col in range(n_col):
-                    @pl.when(jnp.logical_not(mine & (c == col)))
+    def fetch(b):
+        @pl.when(served(seat, b))
+        def _():
+            arrived(right_far, recv_far, b)
+            for col in range(n_col):
+                for other in range(group):
+                    @pl.when(seat != other)
                     def _():
-                        came_far(col, b).wait_recv()
-
-                    for other in range(group):
-                        @pl.when(seat != other)
-                        def _():
-                            to_far_pair(col, b, other).start()
+                        to_far_pair(col, b, other).start()
 
     def answer():
         for other in range(group):
@@ -467,9 +468,14 @@
 
         @pl.when(outer & full)
         def _():
-            for d in range(1, n_fib):
+            for d in range(1, n_fib - 1):
                 pass_up(d, i)
                 pass_down(d, i)
+            partial[...] = products(right, part, jnp.where(has_down, 1, 0), n_fib - 1)
+            pass_up(n_fib - 1, i)
+            pass_down(n_fib - 1, i)
+            total = partial[...] + products(right, part, jnp.where(has_down, 0, n_fib - 1), 1)
+            store(total, own, part, part_out)
 
         if helps:
             @pl.when(helper & (i == ANSWER))
@@ -485,16 +491,20 @@
             def _():
                 reckon(h, 1)
 
+        @pl.when(inner)
+        def _():
+            store(products(right, part, 0, n_fib), own, part, part_out)
+
         @pl.when(full)
         def _():
-            store(products(right, part, 0, n_fib), own, part, part_out)
             for shift in range(1, n_col):
                 to_col(col_at(shift), i).start()
 
         if helps:
-            @pl.when(helper & (i == FETCH))
-            def _():
-                fetch()
+            for b in range(parts):
+                @pl.when(helper & (i == (FIRST_FETCH if b < parts - 1 else FETCH)))
+                def _():
+                    fetch(b)
 
         @pl.when(inner & (i < ANSWER))
         def _():
@@ -599,19 +609,9 @@
                     def _():
                         left_behind(sent_far.at[0], right.at[pl.ds(0, size), across])
 
-            if size and group > 1:
-                @pl.when(helper & (skips(seat, mate) == bool(less)))
-                def _():
-                    left_behind(sent_far_pair.at[0], right.at[pl.ds(0, (group - 1) * size)])
-
-        @pl.when(helper)
-        def _():
-            if lead:
-                if n_col > 1:
-                    left_behind(sent_help.at[0], help_out.at[pl.ds(0, n_col - 1), pl.ds(0, lead * step)])
-                left_behind(sent_done.at[0], helped.at[pl.ds(0, lead * step)])
-            if late:
-                left_behind(sent_owner.at[0], help_out.at[pl.ds(0, n_col), pl.ds(lead * step, late * step)])
+            @pl.when(helper & (skips(seat, mate) == bool(less)))
+            def _():
+                left_behind(sent_helper.at[0], right_far.at[pl.ds(0, (group - 1) * size + few)])
 
 
 def prune(squared_ref, factor_ref, out_hbm, out_vmem, sem):
@@ -662,6 +662,7 @@
                 pltpu.VMEM((n_col, rows, unit), jnp.bfloat16),
                 pltpu.VMEM((8, unit), jnp.float32),
                 pltpu.VMEM((n_row, 1, unit), jnp.float32),
+                pltpu.VMEM((rows // CHUNKS, n_col * unit), jnp.float32),
                 pltpu.VMEM((group * rows, n_col * unit), jnp.bfloat16),
                 pltpu.VMEM((few, unit), jnp.float32),
                 pltpu.VMEM((n_col, few, unit), jnp.bfloat16),
@@ -675,17 +676,14 @@
                 dma((1,)),
                 dma((1,)),
                 dma((1,)),
+                dma((n_fib - 1, CHUNKS)),
+                dma((parts,)),
+                dma((group,)),
+                dma((n_col - 1, CHUNKS // 2)),
                 dma((1,)),
-                dma((1,)),
-                dma((1,)),
-                dma((n_fib - 1, CHUNKS)),
-                dma((n_col, parts)),
+                dma((parts,)),
                 dma((group,)),
-                dma((n_col - 1, CHUNKS)),
-                dma((1,)),
-                dma((n_col, parts)),
-                dma((group,)),
-                dma((n_col - 1, HELP)),
+                dma((n_col - 1, max(HELP - TRAIL, 1))),
                 dma((HELP,)),
             ],
             compiler_params=pltpu.CompilerParams(

time: 44.1 us -> 43.9 us (level)
  no operation moved by 1% of the time
where the time goes in v8:
time: 43.9 us; the launch traced here: 43.7 us
  Pallas kernels  43.7 us (100%)
    pallas_call x1, Pallas kernels, local(): pl.pallas_call(functools.partial(kernel, n_row, n_col, n_fib, helps), out...  42.7 us
    pallas_call x1, Pallas kernels, local(): pl.pallas_call(prune, out_shape=jax.ShapeDtypeStruct((rows, unit), jnp.fl...  1.07 us

profile of v8, /device:TPU:0, one launch (start us, length us, event | category | flops | bytes accessed | tf_op | source)
XLA Modules:
  0.0 43.7 jit_solution(10491383025664055717)
XLA Ops:
  0.0 42.7 %expand.1 = (f32[768,384]{1,0:T(8,128)S(1)}, f32[6,384]{1,0:T(8,128)S(1)}) custom-call(s32[3,6]{1,0:T(4,128)} %bitcast.2, s32[3,6]{1,0:T(4,128)} %bitcast.3, f32[768,384]{1,0:T(8,128)} %values_hbm.1), custom_call_target="tpu_custom_call" | custom-call | tf_op jit(solution)/shard_map/expand/pallas_call | solution.py:640
  42.7 1.1 %prune.1 = f32[768,384]{1,0:T(8,128)} custom-call(f32[768,384]{1,0:T(8,128)S(1)} %get-tuple-element.7.squared_ref, f32[6,384]{1,0:T(8,128)S(1)} %get-tuple-element.8.factor_ref), custom_call_target="tpu_custom_call" | custom-call | tf_op jit(solution)/shard_map/prune/pallas_call | solution.py:694

commit v9 on v8

--- a/solution.py
+++ b/solution.py
@@ -16,6 +16,7 @@
 FETCH = 7
 ANSWER = 9
 LAG = 5
+SLICES = 4
 VMEM_LIMIT = 62 * 1024 * 1024
 
 
@@ -616,15 +617,13 @@
 
 def prune(squared_ref, factor_ref, out_hbm, out_vmem, sem):
     tile = out_vmem.shape[0] // factor_ref.shape[0]
-    copies = []
-    for i in range(factor_ref.shape[0]):
-        down = slice(i * tile, (i + 1) * tile)
-        out_vmem[down] = squared_ref[down] * factor_ref[i:i + 1]
-        copy = pltpu.make_async_copy(out_vmem.at[down], out_hbm.at[down], sem.at[i])
-        copy.start()
-        copies.append(copy)
-    for copy in copies:
-        copy.wait()
+    size = tile // SLICES
+    for i in range(factor_ref.shape[0] * SLICES):
+        down = slice(i * size, (i + 1) * size)
+        at = i // SLICES
+        out_vmem[down] = squared_ref[down] * factor_ref[at:at + 1]
+        pltpu.make_async_copy(out_vmem.at[down], out_hbm.at[down], sem.at[0]).start()
+    pltpu.make_async_copy(out_vmem, out_hbm, sem.at[0]).wait()
 
 
 def solution(mesh):
@@ -701,7 +700,7 @@
             out_specs=pl.BlockSpec(memory_space=pl.ANY),
             scratch_shapes=[
                 pltpu.VMEM((rows, unit), jnp.float32),
-                dma((keep_mask.shape[0],)),
+                dma((1,)),
             ],
             compiler_params=pltpu.CompilerParams(vmem_limit_bytes=8 * 1024 * 1024),
             name="prune",

time: 43.9 us -> 43.8 us (level)
  no operation moved by 1% of the time
where the time goes in v9:
time: 43.8 us; the launch traced here: 43.7 us
  Pallas kernels  43.7 us (100%)
    pallas_call x1, Pallas kernels, local(): pl.pallas_call(functools.partial(kernel, n_row, n_col, n_fib, helps), out...  42.7 us
    pallas_call x1, Pallas kernels, local(): pl.pallas_call(prune, out_shape=jax.ShapeDtypeStruct((rows, unit), jnp.fl...  1 us

profile of v9, /device:TPU:0, one launch (start us, length us, event | category | flops | bytes accessed | tf_op | source)
XLA Modules:
  0.0 43.7 jit_solution(10247649079757125572)
XLA Ops:
  0.0 42.7 %expand.1 = (f32[768,384]{1,0:T(8,128)S(1)}, f32[6,384]{1,0:T(8,128)S(1)}) custom-call(s32[3,6]{1,0:T(4,128)} %bitcast.2, s32[3,6]{1,0:T(4,128)} %bitcast.3, f32[768,384]{1,0:T(8,128)} %values_hbm.1), custom_call_target="tpu_custom_call" | custom-call | tf_op jit(solution)/shard_map/expand/pallas_call | solution.py:639
  42.7 1.0 %prune.1 = f32[768,384]{1,0:T(8,128)} custom-call(f32[768,384]{1,0:T(8,128)S(1)} %get-tuple-element.7.squared_ref, f32[6,384]{1,0:T(8,128)S(1)} %get-tuple-element.8.factor_ref), custom_call_target="tpu_custom_call" | custom-call | tf_op jit(solution)/shard_map/prune/pallas_call | solution.py:693

commit v10 on v9

--- a/solution.py
+++ b/solution.py
@@ -44,13 +44,28 @@
     load_keep.start()
 
     barrier = pltpu.get_barrier_semaphore()
-    for dr in range(n_row):
-        for dc in range(n_col):
-            if dr or dc:
-                pl.semaphore_signal(
-                    barrier, inc=1, device_id_type=MESH,
-                    device_id=(lax.rem(r + dr, n_row), lax.rem(c + dc, n_col), f),
-                )
+
+    def greet(row, col):
+        pl.semaphore_signal(barrier, inc=1, device_id=(row, col, f), device_id_type=MESH)
+
+    for t in range(n_row // group):
+        @pl.when((owner != c) & (owner != t))
+        def _():
+            greet(t * group + seat, owner)
+
+    for dc in range(1, n_col):
+        col = lax.rem(c + dc, n_col)
+
+        @pl.when((owner != c) & (owner != col))
+        def _():
+            greet(c * group + seat, col)
+
+        greet(r, col)
+
+    for dr in range(1, n_row):
+        greet(lax.rem(r + dr, n_row), c)
+
+    peers = n_row + n_col - 2 + jnp.where(owner == c, 0, 2 * n_col - 3)
 
     has_down, has_up = f > 0, f < n_fib - 1
     outer = jnp.logical_not(has_down & has_up)
@@ -77,7 +92,7 @@
             left[f, i * tile:(i + 1) * tile, j * tile:(j + 1) * tile] = masked.astype(jnp.bfloat16)
 
     neighbours = has_down.astype(jnp.int32) + has_up.astype(jnp.int32)
-    pl.semaphore_wait(barrier, n_row * n_col - 1 + neighbours)
+    pl.semaphore_wait(barrier, peers + neighbours)
 
     def chunk(i):
         return pl.ds(i * step if isinstance(i, int) else pl.multiple_of(i * step, step), step)

time: 43.8 us -> 43.8 us (level)
  no operation moved by 1% of the time
where the time goes in v10:
time: 43.8 us; the launch traced here: 43.7 us
  Pallas kernels  43.7 us (100%)
    pallas_call x1, Pallas kernels, local(): pl.pallas_call(functools.partial(kernel, n_row, n_col, n_fib, helps), out...  42.7 us
    pallas_call x1, Pallas kernels, local(): pl.pallas_call(prune, out_shape=jax.ShapeDtypeStruct((rows, unit), jnp.fl...  1 us

profile of v10, /device:TPU:0, one launch (start us, length us, event | category | flops | bytes accessed | tf_op | source)
XLA Modules:
  0.0 43.7 jit_solution(6773794100277541069)
XLA Ops:
  0.0 42.7 %expand.1 = (f32[768,384]{1,0:T(8,128)S(1)}, f32[6,384]{1,0:T(8,128)S(1)}) custom-call(s32[3,6]{1,0:T(4,128)} %bitcast.2, s32[3,6]{1,0:T(4,128)} %bitcast.3, f32[768,384]{1,0:T(8,128)} %values_hbm.1), custom_call_target="tpu_custom_call" | custom-call | tf_op jit(solution)/shard_map/expand/pallas_call | solution.py:654
  42.7 1.0 %prune.1 = f32[768,384]{1,0:T(8,128)} custom-call(f32[768,384]{1,0:T(8,128)S(1)} %get-tuple-element.7.squared_ref, f32[6,384]{1,0:T(8,128)S(1)} %get-tuple-element.8.factor_ref), custom_call_target="tpu_custom_call" | custom-call | tf_op jit(solution)/shard_map/prune/pallas_call | solution.py:708

commit v11 on v10

--- a/solution.py
+++ b/solution.py
@@ -37,7 +37,9 @@
     owner, seat = r // group, lax.rem(r, group)
 
     load = pltpu.make_async_copy(values_hbm, values_ref, load_sem.at[0])
-    load.start()
+    for i in range(rows // tile):
+        down = pl.ds(i * tile, tile)
+        pltpu.make_async_copy(values_hbm.at[down], values_ref.at[down], load_sem.at[0]).start()
     load_tile = pltpu.make_async_copy(tile_hbm, tile_ref, load_sem.at[1])
     load_tile.start()
     load_keep = pltpu.make_async_copy(keep_hbm, keep_ref, load_sem.at[2])

time: 43.8 us -> 43.8 us (level)
  no operation moved by 1% of the time
where the time goes in v11:
time: 43.8 us; the launch traced here: 43.7 us
  Pallas kernels  43.7 us (100%)
    pallas_call x1, Pallas kernels, local(): pl.pallas_call(functools.partial(kernel, n_row, n_col, n_fib, helps), out...  42.7 us
    pallas_call x1, Pallas kernels, local(): pl.pallas_call(prune, out_shape=jax.ShapeDtypeStruct((rows, unit), jnp.fl...  1 us

profile of v11, /device:TPU:0, one launch (start us, length us, event | category | flops | bytes accessed | tf_op | source)
XLA Modules:
  0.0 43.7 jit_solution(9728559827523293146)
XLA Ops:
  0.0 42.7 %expand.1 = (f32[768,384]{1,0:T(8,128)S(1)}, f32[6,384]{1,0:T(8,128)S(1)}) custom-call(s32[3,6]{1,0:T(4,128)} %bitcast.2, s32[3,6]{1,0:T(4,128)} %bitcast.3, f32[768,384]{1,0:T(8,128)} %values_hbm.1), custom_call_target="tpu_custom_call" | custom-call | tf_op jit(solution)/shard_map/expand/pallas_call | solution.py:656
  42.7 1.0 %prune.1 = f32[768,384]{1,0:T(8,128)} custom-call(f32[768,384]{1,0:T(8,128)S(1)} %get-tuple-element.7.squared_ref, f32[6,384]{1,0:T(8,128)S(1)} %get-tuple-element.8.factor_ref), custom_call_target="tpu_custom_call" | custom-call | tf_op jit(solution)/shard_map/prune/pallas_call | solution.py:710

commit v12 on v9

--- a/solution.py
+++ b/solution.py
@@ -12,10 +12,10 @@
 HELP = 3
 TRAIL = 1
 AHEAD = 4
-FIRST_FETCH = 4
+FIRST_FETCH = 3
 FETCH = 7
 ANSWER = 9
-LAG = 5
+LAG = 6
 SLICES = 4
 VMEM_LIMIT = 62 * 1024 * 1024
 

time: 43.8 us -> 43.8 us (level)
  no operation moved by 1% of the time
where the time goes in v12:
time: 43.8 us; the launch traced here: 43.7 us
  Pallas kernels  43.7 us (100%)
    pallas_call x1, Pallas kernels, local(): pl.pallas_call(functools.partial(kernel, n_row, n_col, n_fib, helps), out...  42.7 us
    pallas_call x1, Pallas kernels, local(): pl.pallas_call(prune, out_shape=jax.ShapeDtypeStruct((rows, unit), jnp.fl...  1 us

profile of v12, /device:TPU:0, one launch (start us, length us, event | category | flops | bytes accessed | tf_op | source)
XLA Modules:
  0.0 43.7 jit_solution(1058682316937374891)
XLA Ops:
  0.0 42.7 %expand.1 = (f32[768,384]{1,0:T(8,128)S(1)}, f32[6,384]{1,0:T(8,128)S(1)}) custom-call(s32[3,6]{1,0:T(4,128)} %bitcast.2, s32[3,6]{1,0:T(4,128)} %bitcast.3, f32[768,384]{1,0:T(8,128)} %values_hbm.1), custom_call_target="tpu_custom_call" | custom-call | tf_op jit(solution)/shard_map/expand/pallas_call | solution.py:639
  42.7 1.0 %prune.1 = f32[768,384]{1,0:T(8,128)} custom-call(f32[768,384]{1,0:T(8,128)S(1)} %get-tuple-element.7.squared_ref, f32[6,384]{1,0:T(8,128)S(1)} %get-tuple-element.8.factor_ref), custom_call_target="tpu_custom_call" | custom-call | tf_op jit(solution)/shard_map/prune/pallas_call | solution.py:693
